TPU v7x, 512 devices: a whole 4x8x8 slice. The times are simulated.
512 devices in a mesh: section: 8 (over x, core), expert: 64 (over y, z).
Axes of the slice: x: 4, y: 8, z: 8, core: 2. Of those that a mesh axis runs over, the one named last changes fastest.
Arguments:
- activations: bfloat16 [8, 4096, 3584], P('section', 'expert'), may hold values from -6 to 6
- gradients: bfloat16 [8, 4096, 3584], P('section', 'expert'), may hold values from -6 to 6
- stashed: bfloat16 [2, 8, 4096, 3584], P(None, 'section', 'expert'), may hold values from -6 to 6
- fresh_activations: bfloat16 [1, 4096, 3584], P(None, 'expert'), may hold values from -6 to 6
- fresh_gradients: bfloat16 [1, 4096, 3584], P(None, 'expert'), may hold values from -6 to 6
- w_up: bfloat16 [8, 3584, 8192], P('section', None, 'expert'), may hold values from -0.09375 to 0.09375
- w_down: bfloat16 [8, 8192, 3584], P('section', 'expert'), may hold values from -0.125 to 0.125
- forward_routes: int32 [2, 8, 4096, 8], P(None, 'section', 'expert'), may hold values from 0 to 255, as said below
- forward_gates: float32 [2, 8, 4096, 8], P(None, 'section', 'expert'), may hold values from 0.25 to 2.5
- backward_routes: int32 [2, 8, 4096, 8], P(None, 'section', 'expert'), may hold values from 0 to 255, as said below
- backward_gates: float32 [2, 8, 4096, 8], P(None, 'section', 'expert'), may hold values from 0.25 to 2.5
Outputs:
- section_outputs: bfloat16 [8, 4096, 3584], P('section', 'expert')
- input_gradients: bfloat16 [8, 4096, 3584], P('section', 'expert')
Inputs may be any that keep to these rules, and one draw needn't show every extreme that they name: `forward_routes`: the ids of one token are distinct. For every step and section, no id below 4 is named by more than 3 tokens of one device's block of 64 tokens, and some id below 4 is named by exactly 3 tokens of every device's block. `backward_routes`: the ids of one token are distinct. For every step and section, no id below 4 is named by more than 3 tokens of one device's block of 64 tokens, and some id below 4 is named by exactly 3 tokens of every device's block.
All inputs are finite; a program needn't handle non-finite values.
Results may differ from a plain program's by a relative error of at most 0.005.
Values may be sent and summed in bfloat16 or wider, within the bound.
A program may use at most 64 MiB of HBM per device.

v0:
```python
import jax
import jax.numpy as jnp
from jax import lax
from jax.sharding import PartitionSpec as P

CAP = 3
STEPS = 2
SLICES = 16


def for_sending(shard):
    return jax.tree.map(lambda a: a.astype(jnp.bfloat16) if a.dtype == jnp.float32 else a, shard)


def shifted(shard, axis, by):
    count = lax.axis_size(axis)
    pairs = [(i, i + by) for i in range(count) if 0 <= i + by < count]
    return lax.ppermute(shard, axis, pairs)


def slot_plan(routes, gates, window):
    match = routes[:, :, None] == jnp.arange(window, dtype=jnp.int32)[None, None, :]
    chosen = jnp.sum(match.astype(jnp.float32), axis=1)
    weight = jnp.sum(jnp.where(match, gates[:, :, None], jnp.zeros_like(gates)[:, :, None]), axis=1)
    ranks = jnp.cumsum(chosen, axis=0) - chosen
    places = (ranks[:, :, None] == jnp.arange(CAP, dtype=jnp.float32)[None, None, :]).astype(
        jnp.float32
    )
    return (places * chosen[:, :, None], weight)


def select_rows(places, tokens, devices, window):
    count_tokens, width = tokens.shape
    picker = places.reshape(count_tokens, window * CAP).T.astype(jnp.bfloat16)
    picked = jnp.dot(picker, tokens, preferred_element_type=jnp.float32).astype(jnp.bfloat16)
    spread = jnp.broadcast_to(
        picked.reshape(window, 1, CAP, width), (window, devices // window, CAP, width)
    )
    return spread.reshape(devices, CAP, width)


def combine_rows(returned, places, weight, tokens, window):
    count_tokens, width = tokens.shape
    totals = jnp.sum(returned.reshape(window, -1, CAP, width), axis=1, dtype=jnp.float32)
    scaled = (places * weight[:, :, None]).reshape(count_tokens, window * CAP)
    mixed = jnp.dot(
        scaled,
        totals.reshape(window * CAP, width),
        precision=lax.Precision.HIGHEST,
        preferred_element_type=jnp.float32,
    )
    return (tokens.astype(jnp.float32) + mixed).astype(jnp.bfloat16)


def forward_part(rows, up_slice, down_slice):
    pre = jnp.einsum("snd,dh->snh", rows, up_slice, preferred_element_type=jnp.float32)
    hidden = jax.nn.silu(pre).astype(jnp.bfloat16)
    return jnp.einsum("snh,hd->snd", hidden, down_slice, preferred_element_type=jnp.float32).astype(
        jnp.bfloat16
    )


def backward_part(rows, grad_rows, up_slice, down_slice):
    pre = jnp.einsum("snd,dh->snh", rows, up_slice, preferred_element_type=jnp.float32)
    sigma = jax.nn.sigmoid(pre)
    slope = sigma * (1.0 + pre * (1.0 - sigma))
    dhidden = jnp.einsum("snd,hd->snh", grad_rows, down_slice, preferred_element_type=jnp.float32)
    dpre = (dhidden * slope).astype(jnp.bfloat16)
    return jnp.einsum("snh,dh->snd", dpre, up_slice, preferred_element_type=jnp.float32).astype(
        jnp.bfloat16
    )


def send_back(parts):
    return lax.all_to_all(parts, "expert", split_axis=0, concat_axis=0, tiled=True)


def route(payload, worker):
    return worker(
        jax.tree.map(
            lambda part, own: part.astype(own.dtype),
            lax.all_to_all(for_sending(payload), "expert", split_axis=0, concat_axis=0, tiled=True),
            payload,
        )
    )


def local(
    activations,
    gradients,
    stashed,
    fresh_activations,
    fresh_gradients,
    w_up,
    w_down,
    forward_routes,
    forward_gates,
    backward_routes,
    backward_gates,
):
    devices = lax.axis_size("expert")
    window = devices // SLICES
    section_pos = lax.axis_index("section")
    last_section = lax.axis_size("section") - 1
    up_slice = w_up[0]
    down_slice = w_down[0]

    def ahead_work(rows):
        return send_back(forward_part(rows, up_slice, down_slice))

    def behind_work(pair):
        return send_back(backward_part(pair[0], pair[1], up_slice, down_slice))

    current = activations[0]
    flowing = gradients[0]
    outputs = current
    returned = flowing
    for window_step in range(STEPS):
        places_ahead, weight_ahead = slot_plan(
            forward_routes[window_step, 0], forward_gates[window_step, 0], window
        )
        places_behind, weight_behind = slot_plan(
            backward_routes[window_step, 0], backward_gates[window_step, 0], window
        )
        saved = stashed[window_step, 0]
        send_ahead = select_rows(places_ahead, current, devices, window)
        send_saved = select_rows(places_behind, saved, devices, window)
        send_grads = select_rows(places_behind, flowing, devices, window)
        back_ahead = route(send_ahead, ahead_work)
        back_behind = route((send_saved, send_grads), behind_work)
        outputs = combine_rows(back_ahead, places_ahead, weight_ahead, current, window)
        returned = combine_rows(back_behind, places_behind, weight_behind, flowing, window)
        if window_step + 1 < STEPS:
            moved = shifted(outputs, "section", 1)
            current = jnp.where(section_pos == 0, fresh_activations[window_step], moved)
            arrived = shifted(returned, "section", -1)
            flowing = jnp.where(section_pos == last_section, fresh_gradients[window_step], arrived)
    return (outputs[None], returned[None])


def solution(mesh):
    placed = (
        P("section", "expert", None),
        P("section", "expert", None),
        P(None, "section", "expert", None),
        P(None, "expert", None),
        P(None, "expert", None),
        P("section", None, "expert"),
        P("section", "expert", None),
        P(None, "section", "expert", None),
        P(None, "section", "expert", None),
        P(None, "section", "expert", None),
        P(None, "section", "expert", None),
    )
    return jax.shard_map(
        local,
        mesh=mesh,
        in_specs=placed,
        out_specs=(P("section", "expert", None), P("section", "expert", None)),
        check_vma=False,
    )
```

profile of v0, /device:TPU:6, one launch (start us, length us, event | category | flops | bytes accessed | tf_op | source)
XLA Modules:
  0.0 561.0 jit_solution(15597106591486407782)
XLA Ops:
  0.6 0.8 slice_bitcast_fusion.1
  1.4 0.7 slice_bitcast_fusion
  2.2 0.1 copy.119
  2.3 0.1 reduce_window_sum.27
  2.5 0.1 copy.125
  2.6 0.1 reduce_window_sum.32
  3.0 1.2 convolution_convert_fusion.6
  4.3 1.7 broadcast_in_dim.131
  6.0 16.7 %all-to-all-start.5 = ((bf16[64,3,3584]{2,1,0:T(4,128)(2,1)}), bf16[64,3,3584]{2,1,0:T(4,128)(2,1)S(1)}, u32[]{:S(2)}, u32[]{:S(2)}) async-start(bf16[64,3,3584]{2,1,0:T(4,128)(2,1)} %bitcast.23), calls=%async_computation.5 | async-start | bytes 3670016 | tf_op jit(solution)/shard_map/all_to_all | solution.py:82
  22.8 0.2 convolution_convert_fusion.7
  23.0 46.1 %all-to-all-done.5 = bf16[64,3,3584]{2,1,0:T(4,128)(2,1)S(1)} async-done(((bf16[64,3,3584]{2,1,0:T(4,128)(2,1)}), bf16[64,3,3584]{2,1,0:T(4,128)(2,1)S(1)}, u32[]{:S(2)}, u32[]{:S(2)}) %all-to-all-start.5) | async-done | bytes 1376288 | tf_op jit(solution)/shard_map/all_to_all | solution.py:82
  69.1 1.8 broadcast_in_dim.129
  70.9 10.1 %all-to-all-start.4 = ((bf16[64,3,3584]{2,1,0:T(4,128)(2,1)}), bf16[64,3,3584]{2,1,0:T(4,128)(2,1)S(1)}, u32[]{:S(2)}, u32[]{:S(2)}) async-start(bf16[64,3,3584]{2,1,0:T(4,128)(2,1)} %bitcast.21), calls=%async_computation.4 | async-start | bytes 3670016 | tf_op jit(solution)/shard_map/all_to_all | solution.py:82
  81.0 1.2 convolution_convert_fusion.4
  82.3 43.7 %all-to-all-done.4 = bf16[64,3,3584]{2,1,0:T(4,128)(2,1)S(1)} async-done(((bf16[64,3,3584]{2,1,0:T(4,128)(2,1)}), bf16[64,3,3584]{2,1,0:T(4,128)(2,1)S(1)}, u32[]{:S(2)}, u32[]{:S(2)}) %all-to-all-start.4) | async-done | bytes 1376288 | tf_op jit(solution)/shard_map/all_to_all | solution.py:82
  125.9 1.8 broadcast_in_dim.137
  127.8 9.0 %all-to-all-start.8 = ((bf16[64,3,3584]{2,1,0:T(4,128)(2,1)}), bf16[64,3,3584]{2,1,0:T(4,128)(2,1)}, u32[]{:S(2)}, u32[]{:S(2)}) async-start(bf16[64,3,3584]{2,1,0:T(4,128)(2,1)} %bitcast.30), calls=%async_computation.8 | async-start | bytes 3670016 | tf_op jit(solution)/shard_map/all_to_all | solution.py:82
  136.9 0.1 copy.109
  137.0 0.1 reduce_window_sum.22
  137.2 0.2 convolution_convert_fusion.9
  137.5 43.7 %all-to-all-done.8 = bf16[64,3,3584]{2,1,0:T(4,128)(2,1)} async-done(((bf16[64,3,3584]{2,1,0:T(4,128)(2,1)}), bf16[64,3,3584]{2,1,0:T(4,128)(2,1)}, u32[]{:S(2)}, u32[]{:S(2)}) %all-to-all-start.8) | async-done | bytes 1376288 | tf_op jit(solution)/shard_map/all_to_all | solution.py:82
  181.3 1.8 broadcast_in_dim.120
  183.1 9.3 %all-to-all-start = ((bf16[64,3,3584]{2,1,0:T(4,128)(2,1)}), bf16[64,3,3584]{2,1,0:T(4,128)(2,1)}, u32[]{:S(2)}, u32[]{:S(2)}) async-start(bf16[64,3,3584]{2,1,0:T(4,128)(2,1)} %bitcast.4), calls=%async_computation | async-start | bytes 3670016 | tf_op jit(solution)/shard_map/all_to_all | solution.py:82
  192.4 2.1 fusion.8
  194.5 3.1 convolution_convert_fusion.1
  197.6 2.4 copy.124
  200.0 35.5 %all-to-all-done = bf16[64,3,3584]{2,1,0:T(4,128)(2,1)} async-done(((bf16[64,3,3584]{2,1,0:T(4,128)(2,1)}), bf16[64,3,3584]{2,1,0:T(4,128)(2,1)}, u32[]{:S(2)}, u32[]{:S(2)}) %all-to-all-start) | async-done | bytes 1376288 | tf_op jit(solution)/shard_map/all_to_all | solution.py:82
  235.6 8.8 %all-to-all-start.6 = ((bf16[64,3,3584]{2,1,0:T(4,128)(2,1)}), bf16[64,3,3584]{2,1,0:T(4,128)(2,1)}, u32[]{:S(2)}, u32[]{:S(2)}) async-start(bf16[64,3,3584]{2,1,0:T(4,128)(2,1)} %copy.124), calls=%async_computation.6 | async-start | bytes 3670016 | tf_op jit(solution)/shard_map/all_to_all | solution.py:75
  244.4 2.5 convolution_convert_fusion.3
  246.9 2.5 copy.113
  249.4 38.8 %all-to-all-done.6 = bf16[64,3,3584]{2,1,0:T(4,128)(2,1)} async-done(((bf16[64,3,3584]{2,1,0:T(4,128)(2,1)}), bf16[64,3,3584]{2,1,0:T(4,128)(2,1)}, u32[]{:S(2)}, u32[]{:S(2)}) %all-to-all-start.6) | async-done | bytes 1376288 | tf_op jit(solution)/shard_map/all_to_all | solution.py:75
  288.2 8.8 %all-to-all-start.1 = ((bf16[64,3,3584]{2,1,0:T(4,128)(2,1)}), bf16[64,3,3584]{2,1,0:T(4,128)(2,1)}, u32[]{:S(2)}, u32[]{:S(2)}) async-start(bf16[64,3,3584]{2,1,0:T(4,128)(2,1)} %copy.113), calls=%async_computation.1 | async-start | bytes 3670016 | tf_op jit(solution)/shard_map/all_to_all | solution.py:75
  297.0 2.4 convert_reduce_fusion.1
  299.4 1.7 fusion.2
  301.1 1.9 collective-permute-start.1
  303.1 6.3 %collective-permute-done.1 = bf16[64,3584]{1,0:T(8,128)(2,1)S(1)} collective-permute-done((bf16[64,3584]{1,0:T(8,128)(2,1)}, bf16[64,3584]{1,0:T(8,128)(2,1)S(1)}, u32[]{:S(2)}, u32[]{:S(2)}) %collective-permute-start.1) | collective-permute-done | bytes 458784 | tf_op jit(solution)/shard_map/ppermute | solution.py:18
  309.3 0.2 convolution_convert_fusion.5
  309.6 31.6 %all-to-all-done.1 = bf16[64,3,3584]{2,1,0:T(4,128)(2,1)} async-done(((bf16[64,3,3584]{2,1,0:T(4,128)(2,1)}), bf16[64,3,3584]{2,1,0:T(4,128)(2,1)}, u32[]{:S(2)}, u32[]{:S(2)}) %all-to-all-start.1) | async-done | bytes 1376288 | tf_op jit(solution)/shard_map/all_to_all | solution.py:75
  341.2 1.8 broadcast_in_dim.135
  343.0 8.5 %all-to-all-start.7 = ((bf16[64,3,3584]{2,1,0:T(4,128)(2,1)}), bf16[64,3,3584]{2,1,0:T(4,128)(2,1)}, u32[]{:S(2)}, u32[]{:S(2)}) async-start(bf16[64,3,3584]{2,1,0:T(4,128)(2,1)} %bitcast.140), calls=%async_computation.7 | async-start | bytes 3670016 | tf_op jit(solution)/shard_map/all_to_all | solution.py:82
  351.6 2.4 convert_reduce_fusion.3
  353.9 1.7 fusion.3
  355.7 1.9 collective-permute-start
  357.6 0.1 copy.114
  357.9 7.7 %collective-permute-done = bf16[64,3584]{1,0:T(8,128)(2,1)S(1)} collective-permute-done((bf16[64,3584]{1,0:T(8,128)(2,1)}, bf16[64,3584]{1,0:T(8,128)(2,1)S(1)}, u32[]{:S(2)}, u32[]{:S(2)}) %collective-permute-start) | collective-permute-done | bytes 458784 | tf_op jit(solution)/shard_map/ppermute | solution.py:18
  365.7 0.2 convolution_convert_fusion.8
  366.0 29.9 %all-to-all-done.7 = bf16[64,3,3584]{2,1,0:T(4,128)(2,1)} async-done(((bf16[64,3,3584]{2,1,0:T(4,128)(2,1)}), bf16[64,3,3584]{2,1,0:T(4,128)(2,1)}, u32[]{:S(2)}, u32[]{:S(2)}) %all-to-all-start.7) | async-done | bytes 1376288 | tf_op jit(solution)/shard_map/all_to_all | solution.py:82
  395.9 1.8 broadcast_in_dim.124
  397.7 8.9 %all-to-all-start.2 = ((bf16[64,3,3584]{2,1,0:T(4,128)(2,1)}), bf16[64,3,3584]{2,1,0:T(4,128)(2,1)}, u32[]{:S(2)}, u32[]{:S(2)}) async-start(bf16[64,3,3584]{2,1,0:T(4,128)(2,1)} %bitcast.141), calls=%async_computation.2 | async-start | bytes 3670016 | tf_op jit(solution)/shard_map/all_to_all | solution.py:82
  406.6 2.0 fusion.4
  408.6 3.1 convolution_convert_fusion
  411.8 2.4 copy.130
  414.2 36.4 %all-to-all-done.2 = bf16[64,3,3584]{2,1,0:T(4,128)(2,1)} async-done(((bf16[64,3,3584]{2,1,0:T(4,128)(2,1)}), bf16[64,3,3584]{2,1,0:T(4,128)(2,1)}, u32[]{:S(2)}, u32[]{:S(2)}) %all-to-all-start.2) | async-done | bytes 1376288 | tf_op jit(solution)/shard_map/all_to_all | solution.py:82
  450.6 8.7 %all-to-all-start.9 = ((bf16[64,3,3584]{2,1,0:T(4,128)(2,1)}), bf16[64,3,3584]{2,1,0:T(4,128)(2,1)}, u32[]{:S(2)}, u32[]{:S(2)}) async-start(bf16[64,3,3584]{2,1,0:T(4,128)(2,1)} %copy.130), calls=%async_computation.9 | async-start | bytes 3670016 | tf_op jit(solution)/shard_map/all_to_all | solution.py:75
  459.4 2.5 convolution_convert_fusion.2
  461.9 2.4 copy.118
  464.3 39.1 %all-to-all-done.9 = bf16[64,3,3584]{2,1,0:T(4,128)(2,1)} async-done(((bf16[64,3,3584]{2,1,0:T(4,128)(2,1)}), bf16[64,3,3584]{2,1,0:T(4,128)(2,1)}, u32[]{:S(2)}, u32[]{:S(2)}) %all-to-all-start.9) | async-done | bytes 1376288 | tf_op jit(solution)/shard_map/all_to_all | solution.py:75
  503.3 8.7 %all-to-all-start.3 = ((bf16[64,3,3584]{2,1,0:T(4,128)(2,1)}), bf16[64,3,3584]{2,1,0:T(4,128)(2,1)S(1)}, u32[]{:S(2)}, u32[]{:S(2)}) async-start(bf16[64,3,3584]{2,1,0:T(4,128)(2,1)} %copy.118), calls=%async_computation.3 | async-start | bytes 3670016 | tf_op jit(solution)/shard_map/all_to_all | solution.py:75
  512.1 2.3 convert_reduce_fusion
  514.4 42.0 %all-to-all-done.3 = bf16[64,3,3584]{2,1,0:T(4,128)(2,1)S(1)} async-done(((bf16[64,3,3584]{2,1,0:T(4,128)(2,1)}), bf16[64,3,3584]{2,1,0:T(4,128)(2,1)S(1)}, u32[]{:S(2)}, u32[]{:S(2)}) %all-to-all-start.3) | async-done | bytes 1376288 | tf_op jit(solution)/shard_map/all_to_all | solution.py:75
  556.4 0.8 convert_reduce_fusion.2
  557.2 0.2 copy-done.7
  557.4 1.8 fusion.45
  559.2 1.8 fusion.44
  (74 shorter events, 1.4 us)
Async XLA Ops:
  0.6 191.7 %copy-start = (bf16[1,3584,128]{2,1,0:T(8,128)(2,1)S(1)}, bf16[1,3584,128]{2,1,0:T(8,128)(2,1)}, u32[]{:S(2)}) copy-start(bf16[1,3584,128]{2,1,0:T(8,128)(2,1)} %param.16) | copy-start | bytes 2752516
  6.0 16.7 %copy-start.12 = (bf16[1,64,3584]{2,1,0:T(8,128)(2,1)S(1)}, bf16[1,64,3584]{2,1,0:T(8,128)(2,1)}, u32[]{:S(2)}) copy-start(bf16[1,64,3584]{2,1,0:T(8,128)(2,1)} %param.12) | copy-start | bytes 1376260
  6.0 63.1 %all-to-all-start.5 = ((bf16[64,3,3584]{2,1,0:T(4,128)(2,1)}), bf16[64,3,3584]{2,1,0:T(4,128)(2,1)S(1)}, u32[]{:S(2)}, u32[]{:S(2)}) async-start(bf16[64,3,3584]{2,1,0:T(4,128)(2,1)} %bitcast.23), calls=%async_computation.5 | async-start | bytes 3670016 | tf_op jit(solution)/shard_map/all_to_all | solution.py:82
  69.1 1.8 copy-start.3
  70.9 55.0 %all-to-all-start.4 = ((bf16[64,3,3584]{2,1,0:T(4,128)(2,1)}), bf16[64,3,3584]{2,1,0:T(4,128)(2,1)S(1)}, u32[]{:S(2)}, u32[]{:S(2)}) async-start(bf16[64,3,3584]{2,1,0:T(4,128)(2,1)} %bitcast.21), calls=%async_computation.4 | async-start | bytes 3670016 | tf_op jit(solution)/shard_map/all_to_all | solution.py:82
  125.9 1.8 copy-start.2
  127.8 9.1 %copy-start.16 = (s32[2,1,64,8]{2,3,1,0:T(8,128)S(1)}, s32[2,1,64,8]{2,3,1,0:T(8,128)}, u32[]{:S(2)}) copy-start(s32[2,1,64,8]{2,3,1,0:T(8,128)} %param.18) | copy-start | bytes 12292
  127.8 9.1 %copy-start.17 = (f32[2,1,64,8]{2,3,1,0:T(8,128)S(1)}, f32[2,1,64,8]{2,3,1,0:T(8,128)}, u32[]{:S(2)}) copy-start(f32[2,1,64,8]{2,3,1,0:T(8,128)} %param.19) | copy-start | bytes 12292
  127.8 9.4 %copy-start.14 = (bf16[1,64,3584]{2,1,0:T(8,128)(2,1)S(1)}, bf16[1,64,3584]{2,1,0:T(8,128)(2,1)}, u32[]{:S(2)}) copy-start(bf16[1,64,3584]{2,1,0:T(8,128)(2,1)} %param.11) | copy-start | bytes 1376260
  127.8 53.5 %all-to-all-start.8 = ((bf16[64,3,3584]{2,1,0:T(4,128)(2,1)}), bf16[64,3,3584]{2,1,0:T(4,128)(2,1)}, u32[]{:S(2)}, u32[]{:S(2)}) async-start(bf16[64,3,3584]{2,1,0:T(4,128)(2,1)} %bitcast.30), calls=%async_computation.8 | async-start | bytes 3670016 | tf_op jit(solution)/shard_map/all_to_all | solution.py:82
  183.1 52.5 %all-to-all-start = ((bf16[64,3,3584]{2,1,0:T(4,128)(2,1)}), bf16[64,3,3584]{2,1,0:T(4,128)(2,1)}, u32[]{:S(2)}, u32[]{:S(2)}) async-start(bf16[64,3,3584]{2,1,0:T(4,128)(2,1)} %bitcast.4), calls=%async_computation | async-start | bytes 3670016 | tf_op jit(solution)/shard_map/all_to_all | solution.py:82
  192.3 2.1 copy-start.1
  235.6 52.6 %all-to-all-start.6 = ((bf16[64,3,3584]{2,1,0:T(4,128)(2,1)}), bf16[64,3,3584]{2,1,0:T(4,128)(2,1)}, u32[]{:S(2)}, u32[]{:S(2)}) async-start(bf16[64,3,3584]{2,1,0:T(4,128)(2,1)} %copy.124), calls=%async_computation.6 | async-start | bytes 3670016 | tf_op jit(solution)/shard_map/all_to_all | solution.py:75
  288.2 53.0 %all-to-all-start.1 = ((bf16[64,3,3584]{2,1,0:T(4,128)(2,1)}), bf16[64,3,3584]{2,1,0:T(4,128)(2,1)}, u32[]{:S(2)}, u32[]{:S(2)}) async-start(bf16[64,3,3584]{2,1,0:T(4,128)(2,1)} %copy.113), calls=%async_computation.1 | async-start | bytes 3670016 | tf_op jit(solution)/shard_map/all_to_all | solution.py:75
  297.0 2.4 copy-start.13
  297.0 12.3 %copy-start.4 = (bf16[1,64,3584]{2,1,0:T(8,128)(2,1)S(1)}, bf16[1,64,3584]{2,1,0:T(8,128)(2,1)}, u32[]{:S(2)}) copy-start(bf16[1,64,3584]{2,1,0:T(8,128)(2,1)} %param.15) | copy-start | bytes 1376260
  301.1 8.2 %collective-permute-start.1 = (bf16[64,3584]{1,0:T(8,128)(2,1)}, bf16[64,3584]{1,0:T(8,128)(2,1)S(1)}, u32[]{:S(2)}, u32[]{:S(2)}) collective-permute-start(bf16[64,3584]{1,0:T(8,128)(2,1)} %fusion.2), channel_id=1, source_target_pairs={{64,0},{128,64},{192,128},{256,192},{320,256},{384,320},{448,384},... | collective-permute-start | bytes 1376264 | tf_op jit(solution)/shard_map/ppermute | solution.py:18
  309.3 33.6 %copy-start.6 = (bf16[64,3584]{1,0:T(8,128)(2,1)}, bf16[64,3584]{1,0:T(8,128)(2,1)S(1)}, u32[]{:S(2)}) copy-start(bf16[64,3584]{1,0:T(8,128)(2,1)S(1)} %collective-permute-done.1) | copy-start | bytes 1376260
  343.0 52.9 %all-to-all-start.7 = ((bf16[64,3,3584]{2,1,0:T(4,128)(2,1)}), bf16[64,3,3584]{2,1,0:T(4,128)(2,1)}, u32[]{:S(2)}, u32[]{:S(2)}) async-start(bf16[64,3,3584]{2,1,0:T(4,128)(2,1)} %bitcast.140), calls=%async_computation.7 | async-start | bytes 3670016 | tf_op jit(solution)/shard_map/all_to_all | solution.py:82
  351.5 2.4 copy-start.15
  351.5 14.1 %copy-start.8 = (bf16[1,64,3584]{2,1,0:T(8,128)(2,1)S(1)}, bf16[1,64,3584]{2,1,0:T(8,128)(2,1)}, u32[]{:S(2)}) copy-start(bf16[1,64,3584]{2,1,0:T(8,128)(2,1)} %param.14) | copy-start | bytes 1376260
  355.7 10.0 %collective-permute-start = (bf16[64,3584]{1,0:T(8,128)(2,1)}, bf16[64,3584]{1,0:T(8,128)(2,1)S(1)}, u32[]{:S(2)}, u32[]{:S(2)}) collective-permute-start(bf16[64,3584]{1,0:T(8,128)(2,1)} %fusion.3), channel_id=1, source_target_pairs={{0,64},{64,128},{128,192},{192,256},{256,320},{320,384},{384,448},... | collective-permute-start | bytes 1376264 | tf_op jit(solution)/shard_map/ppermute | solution.py:18
  365.7 32.0 %copy-start.10 = (bf16[64,3584]{1,0:T(8,128)(2,1)}, bf16[64,3584]{1,0:T(8,128)(2,1)S(1)}, u32[]{:S(2)}) copy-start(bf16[64,3584]{1,0:T(8,128)(2,1)S(1)} %collective-permute-done) | copy-start | bytes 1376260
  397.7 53.0 %all-to-all-start.2 = ((bf16[64,3,3584]{2,1,0:T(4,128)(2,1)}), bf16[64,3,3584]{2,1,0:T(4,128)(2,1)}, u32[]{:S(2)}, u32[]{:S(2)}) async-start(bf16[64,3,3584]{2,1,0:T(4,128)(2,1)} %bitcast.141), calls=%async_computation.2 | async-start | bytes 3670016 | tf_op jit(solution)/shard_map/all_to_all | solution.py:82
  450.6 52.7 %all-to-all-start.9 = ((bf16[64,3,3584]{2,1,0:T(4,128)(2,1)}), bf16[64,3,3584]{2,1,0:T(4,128)(2,1)}, u32[]{:S(2)}, u32[]{:S(2)}) async-start(bf16[64,3,3584]{2,1,0:T(4,128)(2,1)} %copy.130), calls=%async_computation.9 | async-start | bytes 3670016 | tf_op jit(solution)/shard_map/all_to_all | solution.py:75
  503.3 53.1 %all-to-all-start.3 = ((bf16[64,3,3584]{2,1,0:T(4,128)(2,1)}), bf16[64,3,3584]{2,1,0:T(4,128)(2,1)S(1)}, u32[]{:S(2)}, u32[]{:S(2)}) async-start(bf16[64,3,3584]{2,1,0:T(4,128)(2,1)} %copy.118), calls=%async_computation.3 | async-start | bytes 3670016 | tf_op jit(solution)/shard_map/all_to_all | solution.py:75
  512.1 45.1 %copy-start.5 = (bf16[1,64,3584]{2,1,0:T(8,128)(2,1)S(1)}, bf16[1,64,3584]{2,1,0:T(8,128)(2,1)}, u32[]{:S(2)}) copy-start(bf16[1,64,3584]{2,1,0:T(8,128)(2,1)} %param.15) | copy-start | bytes 1376260
  556.4 1.0 copy-start.7
  556.4 2.8 copy-start.9
  556.4 2.8 copy-start.11
where the time goes:
time: 564 us; the launch traced here: 561 us
  waiting for transfers between devices  401 us (71%)
  starting transfers between devices  101 us (18%)
  matrix products  25.7 us (5%)
  local copies, waits for them, and re-layouts  23.6 us (4%)
  other arithmetic  8.42 us (1%)
    all_to_all x6, waiting for transfers between devices, route(): lax.all_to_all(for_sending(payload), 'expert', split_axis=0, concat_axis=...  235 us
    all_to_all x4, waiting for transfers between devices, send_back(): lax.all_to_all(parts, 'expert', split_axis=0, concat_axis=0, tiled=True)  151 us
    all_to_all x6, starting transfers between devices, route(): lax.all_to_all(for_sending(payload), 'expert', split_axis=0, concat_axis=...  62.5 us
    all_to_all x4, starting transfers between devices, send_back(): lax.all_to_all(parts, 'expert', split_axis=0, concat_axis=0, tiled=True)  35.1 us
    ppermute x2, waiting for transfers between devices, shifted(): return lax.ppermute(shard, axis, pairs)  14 us
  transfers between devices with their start and end apart: 12, of which 12 were waited for; matrix products, arithmetic and copies ran while one was open for 7% of the time, Pallas kernels for 0%

commit v1 on v0

v1 whole, which is shorter than its diff:
```python
import jax
import jax.numpy as jnp
import numpy as np
from jax import lax
from jax.experimental import pallas as pl
from jax.experimental.pallas import tpu as pltpu
from jax.sharding import PartitionSpec as P

CAP = 3
STEPS = 2
WINDOW = 4
TOK = 64
D = 3584
W = D // 2
C = W // 2
HID_DEV = 128
NY = 8
NZ = 8
PAD = 16
ROWS = 3 * NY * CAP
BACK = 2 * NY * CAP
HALF = NY * CAP
BF = jnp.bfloat16
F32 = jnp.float32
TRANS = (((1,), (1,)), ((), ()))
FAR_FIRST = (4, 3, 5, 2, 6, 1, 7)


def dot(a, b):
    return jnp.dot(a, b, preferred_element_type=F32)


def dot_t(a, b):
    return lax.dot_general(a, b, TRANS, preferred_element_type=F32)


def kernel(x_in, g_in, st_in, fx_in, fg_in, up_in, dn_in, pk_in, sc_in, cmp_in, exp_in,
           out_ref, dx_ref,
           xs, gs, upf, dnf, upc, sendy, ybuf, zbuf, pp, xsend, xrecv, pbuf, ra, rb, rsend, ret,
           w_ss, w_rs, y_ss, y_rs, za_ss, za_rs, zb_ss, zb_rs, e_ss, e_rs,
           ra_ss, ra_rs, rb_ss, rb_rs, t_ss, t_rs, s_ss, s_rs):
    sec = lax.axis_index("section")
    me = lax.axis_index("expert")
    y = me // NZ
    z = me % NZ
    par = y % 2
    mate = (y + 1 - 2 * par) * NZ + z
    flip = sec % 2
    sgn = 1 - 2 * flip
    to_a = y * NZ + (z + sgn + NZ) % NZ
    to_b = y * NZ + (z - sgn + NZ) % NZ
    sec_up = (sec + 1) % 8
    sec_dn = (sec + 7) % 8

    def at(block):
        return (block + 2 * NZ) % NZ

    def remote(src, dst, ss, rs, expert, section=None):
        return pltpu.make_async_remote_copy(
            src_ref=src, dst_ref=dst, send_sem=ss, recv_sem=rs,
            device_id=(sec if section is None else section, expert),
            device_id_type=pl.DeviceIdType.MESH)

    barrier = pltpu.get_barrier_semaphore()
    peers = [(sec, ((y + k) % NY) * NZ + z) for k in range(1, NY)]
    peers += [(sec, to_a), (sec, to_b), (sec_up, me), (sec_dn, me)]
    for peer in peers:
        pl.semaphore_signal(barrier, inc=1, device_id=peer, device_id_type=pl.DeviceIdType.MESH)
    xs[0] = x_in[...]
    gs[0] = g_in[...]
    pl.semaphore_wait(barrier, len(peers))

    def weight_copies():
        return (
            remote(up_in.at[1 - par], upf.at[par], w_ss.at[0], w_rs.at[0], mate),
            remote(dn_in.at[1 - par], dnf.at[par], w_ss.at[1], w_rs.at[1], mate),
        )

    def step(t, carry):
        @pl.when(t == 1)
        def _():
            up_shift, dn_shift = shift_copies()
            up_shift.wait()
            dn_shift.wait()

            @pl.when(sec == 0)
            def _():
                xs[1] = fx_in[...]

            @pl.when(sec == 7)
            def _():
                gs[1] = fg_in[...]

        picked = dot(pk_in[t, 0], xs[t]) + dot(pk_in[t, 1], st_in[t]) + dot(pk_in[t, 2], gs[t])
        picked = picked.astype(BF)
        for e in range(WINDOW):
            for half in range(2):
                sendy[t, 2 * e + half] = picked[e * PAD:(e + 1) * PAD, half * W:(half + 1) * W]
        sent_y = []
        for k in FAR_FIRST:
            to = (y + k) % NY
            copy = remote(sendy.at[t, to], ybuf.at[t, y], y_ss.at[t, k], y_rs.at[t, k], to * NZ + z)
            copy.start()
            sent_y.append(copy)
        ybuf[t, y] = sendy[t, y]
        for copy in sent_y:
            copy.wait_recv()

        @pl.when(t == 0)
        def _():
            for copy in weight_copies():
                copy.start()

        block = dot(cmp_in[...], ybuf[t].reshape(NY * PAD, W)).astype(BF)
        for c in range(2):
            zbuf[t, z, c] = block[:, c * C:(c + 1) * C]

        def go_a(h, c):
            b = at(z - sgn * h)
            return remote(zbuf.at[t, b, c], zbuf.at[t, b, c], za_ss.at[t, h, c], za_rs.at[t, h, c], to_a)

        def go_b(h, c):
            b = at(z + sgn * h)
            return remote(zbuf.at[t, b, c], zbuf.at[t, b, c], zb_ss.at[t, h, c], zb_rs.at[t, h, c], to_b)

        def swap(b):
            return remote(xsend.at[t, b], xrecv.at[t, b], e_ss.at[t, b], e_rs.at[t, b], mate)

        def first_half(b):
            rows = [zbuf[t, b, c] for c in range(2)]
            pre = dot(rows[0][:BACK], upc[:C]) + dot(rows[1][:BACK], upc[C:])
            down = dnf[...].reshape(2 * HID_DEV, W)
            dh = dot_t(rows[0][BACK:], down[:, :C]) + dot_t(rows[1][BACK:], down[:, C:])
            both = jnp.concatenate([pre, dh], axis=0)
            pp[t, b] = both
            xsend[t, b] = both.astype(BF)
            swap(b).start()

        for c in range(2):
            go_a(0, c).start()
            go_b(0, c).start()
        for h in range(4):
            for c in range(2):
                go_a(h, c).wait_recv()
                if h < 3:
                    go_a(h + 1, c).start()
                    go_b(h, c).wait_recv()
                    if h < 2:
                        go_b(h + 1, c).start()
            if h == 1:
                @pl.when(t == 0)
                def _():
                    upf[par] = up_in[par]
                    dnf[par] = dn_in[par]
                    for copy in weight_copies():
                        copy.wait()
                    upc[:, :HID_DEV] = upf[0]
                    upc[:, HID_DEV:] = upf[1]

                first_half(z)
                first_half(at(z - sgn))
                first_half(at(z + sgn))
            if h >= 1:
                first_half(at(z - sgn * (h + 1)))
                if h < 3:
                    first_half(at(z + sgn * (h + 1)))

        def second_half(b):
            swap(b).wait_recv()
            both = pp[t, b] + xrecv[t, b].astype(F32)
            v = both[:HALF]
            hidden = (v / (1.0 + jnp.exp(-v))).astype(BF)
            u = both[HALF:BACK]
            sigma = 1.0 / (1.0 + jnp.exp(-u))
            dpre = (both[BACK:] * (sigma * (1.0 + u * (1.0 - sigma)))).astype(BF)
            part = dot(hidden, dnf[...].reshape(2 * HID_DEV, W))
            for c in range(2):
                dpart = dot_t(dpre, upc[c * C:(c + 1) * C])
                pbuf[t, b, c] = jnp.concatenate([part[:, c * C:(c + 1) * C], dpart], axis=0).astype(BF)

        def back_a(h, c):
            b = at(z + sgn * (4 - h))
            return remote(pbuf.at[t, b, c], ra.at[t, h, c], ra_ss.at[t, h, c], ra_rs.at[t, h, c], to_a)

        def back_b(h, c):
            b = at(z - sgn * (3 - h))
            return remote(pbuf.at[t, b, c], rb.at[t, h, c], rb_ss.at[t, h, c], rb_rs.at[t, h, c], to_b)

        for h in range(4):
            b = at(z + sgn * (4 - h))
            second_half(b)
            for c in range(2):
                if h > 0:
                    back_a(h - 1, c).wait_recv()
                    pbuf[t, b, c] = (pbuf[t, b, c].astype(F32) + ra[t, h - 1, c].astype(F32)).astype(BF)
                back_a(h, c).start()
            if h < 3:
                b = at(z - sgn * (3 - h))
                second_half(b)
                for c in range(2):
                    if h > 0:
                        back_b(h - 1, c).wait_recv()
                        pbuf[t, b, c] = (pbuf[t, b, c].astype(F32) + rb[t, h - 1, c].astype(F32)).astype(BF)
                    back_b(h, c).start()
        second_half(z)
        for c in range(2):
            back_b(2, c).wait_recv()
            back_a(3, c).wait_recv()
            total = (pbuf[t, z, c].astype(F32) + ra[t, 3, c].astype(F32) + rb[t, 2, c].astype(F32)).astype(BF)
            spread = dot(exp_in[...], total).astype(BF)
            for k in range(NY):
                rsend[t, k, :, c * C:(c + 1) * C] = spread[k * 8:(k + 1) * 8]
        sent_t = []
        for k in FAR_FIRST:
            to = (y + k) % NY
            copy = remote(rsend.at[t, to], ret.at[t, y], t_ss.at[t, k], t_rs.at[t, k], to * NZ + z)
            copy.start()
            sent_t.append(copy)
        ret[t, y] = rsend[t, y]
        for copy in sent_t:
            copy.wait_recv()
        for half in range(2):
            totals = jnp.concatenate([ret[t, 2 * e + half].astype(F32) for e in range(WINDOW)], axis=0)
            cols = slice(half * W, (half + 1) * W)
            for ref, own, which in ((out_ref, xs, 0), (dx_ref, gs, 1)):
                mixed = jnp.dot(sc_in[t, which], totals, precision=lax.Precision.HIGHEST,
                                preferred_element_type=F32)
                ref[:, cols] = (own[t, :, cols].astype(F32) + mixed).astype(BF)

        @pl.when(t == 0)
        def _():
            for copy in shift_copies():
                copy.start()

        for copy in sent_y + sent_t:
            copy.wait_send()
        for c in range(2):
            for h in range(4):
                go_a(h, c).wait_send()
                back_a(h, c).wait_send()
            for h in range(3):
                go_b(h, c).wait_send()
                back_b(h, c).wait_send()
        for b in range(NZ):
            swap(b).wait_send()
        return carry

    def shift_copies():
        return (
            remote(out_ref, xs.at[1], s_ss.at[0], s_rs.at[0], me, sec_up),
            remote(dx_ref, gs.at[1], s_ss.at[1], s_rs.at[1], me, sec_dn),
        )

    lax.fori_loop(0, STEPS, step, 0)


def slot_plan(routes, gates):
    match = routes[..., None] == jnp.arange(WINDOW, dtype=jnp.int32)
    chosen = jnp.sum(match.astype(F32), axis=2)
    weight = jnp.sum(jnp.where(match, gates[..., None], 0.0), axis=2)
    ranks = jnp.cumsum(chosen, axis=1) - chosen
    places = (ranks[..., None] == jnp.arange(CAP, dtype=F32)).astype(F32)
    return places * chosen[..., None], weight


def plans(fr, fg, br, bg):
    pf, wf = slot_plan(fr, fg)
    pb, wb = slot_plan(br, bg)

    def picker(places, s):
        m = jnp.transpose(places, (0, 2, 3, 1))
        m = jnp.pad(m, ((0, 0), (0, 0), (s * CAP, PAD - (s + 1) * CAP), (0, 0)))
        return m.reshape(STEPS, WINDOW * PAD, TOK).astype(BF)

    def scaler(places, weight, s):
        m = places * weight[..., None]
        m = jnp.pad(m, ((0, 0), (0, 0), (0, 0), (s * CAP, 8 - (s + 1) * CAP)))
        return m.reshape(STEPS, TOK, WINDOW * 8)

    pick = jnp.stack([picker(pf, 0), picker(pb, 1), picker(pb, 2)], axis=1)
    scale = jnp.stack([scaler(pf, wf, 0), scaler(pb, wb, 1)], axis=1)
    return pick, scale


def constants():
    i = np.arange(ROWS)
    j = np.arange(NY * PAD)
    s, k, c = i // HALF, (i % HALF) // CAP, i % CAP
    squeeze = ((k * PAD + s * CAP + c)[:, None] == j[None, :])
    i = np.arange(BACK)
    s, k, c = i // HALF, (i % HALF) // CAP, i % CAP
    spread = (np.arange(NY * 8)[:, None] == (k * 8 + s * CAP + c)[None, :])
    return jnp.asarray(squeeze, BF), jnp.asarray(spread, BF)


def local(activations, gradients, stashed, fresh_activations, fresh_gradients, w_up, w_down,
          forward_routes, forward_gates, backward_routes, backward_gates):
    pick, scale = plans(forward_routes[:, 0], forward_gates[:, 0], backward_routes[:, 0], backward_gates[:, 0])
    squeeze, spread = constants()
    up = w_up[0].reshape(2, W, HID_DEV)
    down = jnp.stack([w_down[0][:, :W], w_down[0][:, W:]])
    vmem = pl.BlockSpec(memory_space=pltpu.VMEM)
    dma = pltpu.SemaphoreType.DMA
    shape = jax.ShapeDtypeStruct((TOK, D), BF)
    S = STEPS
    out, dx = pl.pallas_call(
        kernel,
        out_shape=(shape, shape),
        in_specs=[vmem] * 11,
        out_specs=(vmem, vmem),
        scratch_shapes=[
            pltpu.VMEM((S, TOK, D), BF),
            pltpu.VMEM((S, TOK, D), BF),
            pltpu.VMEM((2, W, HID_DEV), BF),
            pltpu.VMEM((2, HID_DEV, W), BF),
            pltpu.VMEM((W, 2 * HID_DEV), BF),
            pltpu.VMEM((S, NY, PAD, W), BF),
            pltpu.VMEM((S, NY, PAD, W), BF),
            pltpu.VMEM((S, NZ, 2, ROWS, C), BF),
            pltpu.VMEM((S, NZ, ROWS, 2 * HID_DEV), F32),
            pltpu.VMEM((S, NZ, ROWS, 2 * HID_DEV), BF),
            pltpu.VMEM((S, NZ, ROWS, 2 * HID_DEV), BF),
            pltpu.VMEM((S, NZ, 2, BACK, C), BF),
            pltpu.VMEM((S, 4, 2, BACK, C), BF),
            pltpu.VMEM((S, 3, 2, BACK, C), BF),
            pltpu.VMEM((S, NY, 8, W), BF),
            pltpu.VMEM((S, NY, 8, W), BF),
            dma((2,)), dma((2,)),
            dma((S, NY)), dma((S, NY)),
            dma((S, 4, 2)), dma((S, 4, 2)),
            dma((S, 3, 2)), dma((S, 3, 2)),
            dma((S, NZ)), dma((S, NZ)),
            dma((S, 4, 2)), dma((S, 4, 2)),
            dma((S, 3, 2)), dma((S, 3, 2)),
            dma((S, NY)), dma((S, NY)),
            dma((2,)), dma((2,)),
        ],
        compiler_params=pltpu.CompilerParams(
            collective_id=0, has_side_effects=True, vmem_limit_bytes=60 * 1024 * 1024),
    )(activations[0], gradients[0], stashed[:, 0], fresh_activations[0], fresh_gradients[0],
      up, down, pick, scale, squeeze, spread)
    return out[None], dx[None]


def solution(mesh):
    placed = (
        P("section", "expert", None),
        P("section", "expert", None),
        P(None, "section", "expert", None),
        P(None, "expert", None),
        P(None, "expert", None),
        P("section", None, "expert"),
        P("section", "expert", None),
        P(None, "section", "expert", None),
        P(None, "section", "expert", None),
        P(None, "section", "expert", None),
        P(None, "section", "expert", None),
    )
    return jax.shard_map(
        local,
        mesh=mesh,
        in_specs=placed,
        out_specs=(P("section", "expert", None), P("section", "expert", None)),
        check_vma=False,
    )
```

time: 564 us -> 174 us (0.31)
  waiting for transfers between devices: 401 us -> 0 us
  Pallas kernels: 0 us -> 164 us
  starting transfers between devices: 101 us -> 0 us
  matrix products: 25.7 us -> 0 us
  local copies, waits for them, and re-layouts: 23.6 us -> 5.02 us
  other arithmetic: 8.42 us -> 2.71 us
    all_to_all x10 -> x0, waiting for transfers between devices: 387 us -> none  [the longest x6 235 us: route(): lax.all_to_all(for_sending(payload), 'expert', split_axis=0, concat_axis=...]
    pallas_call x0 -> x1, Pallas kernels: none -> 164 us  [local(): pl.pallas_call(kernel, out_shape=(shape, shape), in_specs=[vmem] * 11, ou...]
    all_to_all x10 -> x0, starting transfers between devices: 97.6 us -> none  [the longest x6 62.5 us: route(): lax.all_to_all(for_sending(payload), 'expert', split_axis=0, concat_axis=...]
    dot_general x16 -> x0, matrix products: 25.7 us -> none  [the longest x4 7.02 us: combine_rows(): jnp.dot(scaled, totals.reshape(window * CAP, width), precision=lax.Precis...]
    ppermute x2 -> x0, waiting for transfers between devices: 14 us -> none  [shifted(): return lax.ppermute(shard, axis, pairs)]
    broadcast_in_dim x14 -> x0, local copies, waits for them, and re-layouts: 11.9 us -> none  [the longest x12 11.2 us: select_rows(): jnp.broadcast_to(picked.reshape(window, 1, CAP, width), (window, devices...]
    convert_element_type x4 -> x0, local copies, waits for them, and re-layouts: 9.73 us -> none  [the longest x2 4.87 us: forward_part(): jnp.einsum('snh,hd->snd', hidden, down_slice, preferred_element_type=jnp....]
    reduce_sum x7 -> x2, other arithmetic: 7.93 us -> 0.07 us  [slot_plan(): weight = jnp.sum(jnp.where(match, gates[..., None], 0.0), axis=2)]
  transfers between devices with their start and end apart: 12 -> 0, of which waited for: 12 -> 0; matrix products, arithmetic and copies ran while one was open for 7% -> 0% of each run, Pallas kernels for 0% -> 0%
where the time goes in v1:
time: 174 us; the launch traced here: 173 us
  Pallas kernels  164 us (94%)
  local copies, waits for them, and re-layouts  5.02 us (3%)
  other arithmetic  2.71 us (2%)
    pallas_call x1, Pallas kernels, local(): pl.pallas_call(kernel, out_shape=(shape, shape), in_specs=[vmem] * 11, ou...  164 us
    unnamed x14, local copies, waits for them, and re-layouts  4.02 us

profile of v1, /device:TPU:6, one launch (start us, length us, event | category | flops | bytes accessed | tf_op | source)
XLA Modules:
  0.0 172.7 jit_solution(4584336458335012018)
XLA Ops:
  0.6 0.0 copy-start.3
  0.6 0.0 copy-start.2
  0.7 0.7 copy-done.3
  1.3 0.0 copy-done.2
  1.3 0.0 copy-start.4
  1.3 0.0 copy-start.5
  1.4 0.7 copy-done.4
  2.0 0.0 copy-done.5
  2.1 0.1 copy.41
  2.2 0.1 copy.44
  2.3 0.1 copy.37
  2.4 0.1 copy.40
  2.5 0.1 reduce_window_sum.21
  2.6 0.1 reduce_window_sum.23
  2.7 0.0 copy-start
  2.8 0.1 copy.43
  2.8 0.1 copy.48
  3.0 0.1 copy.50
  3.1 0.1 copy.39
  3.2 0.1 copy.46
  3.4 0.7 pad_maximum_fusion.2.pk_in
  4.0 0.1 copy.49
  4.1 0.7 pad_maximum_fusion.1.sc_in
  4.8 0.0 copy-done
  4.8 0.1 slice_bitcast_fusion.1
  4.9 1.0 pad_maximum_fusion.dn_in
  5.9 164.2 %shard_map.140 = (bf16[64,3584]{1,0:T(8,128)(2,1)}, bf16[64,3584]{1,0:T(8,128)(2,1)}) custom-call(bf16[64,3584]{1,0:T(8,128)(2,1)} %bitcast.37, bf16[64,3584]{1,0:T(8,128)(2,1)} %bitcast.38, bf16[2,64,3584]{2,1,0:T(8,128)(2,1)} %bitcast.35, bf16[64,3584]{1,0:T(8,128)(2,1)} %bitcast.39, bf16[64,3584]{1,0:T(8,128)(2,1)} %bitcast.40, ...), custom_call_target="tpu_custom_call" | custom-call | tf_op jit(solution)/shard_map/pallas_call | solution.py:306
  170.1 0.0 copy-start.1
  170.1 1.9 %copy.53 = bf16[1,64,3584]{2,1,0:T(8,128)(2,1)} copy(bf16[1,64,3584]{2,1,0:T(8,128)(2,1)} %bitcast.42) | data formatting | bytes 917504
  172.0 0.0 copy-done.1
  172.0 0.8 copy.54
  (14 shorter events, 0.2 us)
Async XLA Ops:
  0.6 0.7 copy-start.3
  0.6 0.7 copy-start.2
  1.3 0.7 copy-start.4
  1.3 0.7 copy-start.5
  2.7 2.1 %copy-start = (bf16[1,128,3584]{2,1,0:T(8,128)(2,1)S(1)}, bf16[1,128,3584]{2,1,0:T(8,128)(2,1)}, u32[]{:S(2)}) copy-start(bf16[1,128,3584]{2,1,0:T(8,128)(2,1)} %param.19) | copy-start | bytes 2752516
  170.1 1.9 %copy-start.1 = (bf16[64,3584]{1,0:T(8,128)(2,1)S(1)}, bf16[64,3584]{1,0:T(8,128)(2,1)}, u32[]{:S(2)}) copy-start(bf16[64,3584]{1,0:T(8,128)(2,1)} %get-tuple-element.5) | copy-start | bytes 1376260

commit v2 on v1

v2 whole, which is shorter than its diff:
```python
import jax
import jax.numpy as jnp
import numpy as np
from jax import lax
from jax.experimental import pallas as pl
from jax.experimental.pallas import tpu as pltpu
from jax.sharding import PartitionSpec as P

CAP = 3
STEPS = 2
WINDOW = 4
TOK = 64
D = 3584
W = D // 2
C = W // 2
HID_DEV = 128
NY = 8
NZ = 8
PAD = 16
ROWS = 3 * NY * CAP
BACK = 2 * NY * CAP
HALF = NY * CAP
BF = jnp.bfloat16
F32 = jnp.float32
TRANS = (((1,), (1,)), ((), ()))
FAR_FIRST = (4, 3, 5, 2, 6, 1, 7)


def dot(a, b):
    return jnp.dot(a, b, preferred_element_type=F32)


def dot_t(a, b):
    return lax.dot_general(a, b, TRANS, preferred_element_type=F32)


def kernel(x_in, g_in, st_in, fx_in, fg_in, up_in, dn_in, pk0_in, pk1_in, sc_in, cmp0_in, cmp1_in, exp_in,
           out_ref, dx_ref,
           shout, land, upf, dnf, upc, sendy0, ybuf0, sendy1, ybuf1, zbuf0, zbuf1, zsave, pp, xsend, xrecv,
           pbuf, ra, rb, rsend, ret,
           w_ss, w_rs, y_ss, y_rs, za_ss, za_rs, zb_ss, zb_rs, va_ss, va_rs, vb_ss, vb_rs, e_ss, e_rs,
           ra_ss, ra_rs, rb_ss, rb_rs, t_ss, t_rs, s_ss, s_rs):
    sec = lax.axis_index("section")
    me = lax.axis_index("expert")
    y = me // NZ
    z = me % NZ
    par = y % 2
    mate = (y + 1 - 2 * par) * NZ + z
    flip = sec % 2
    sgn = 1 - 2 * flip
    to_a = y * NZ + (z + sgn + NZ) % NZ
    to_b = y * NZ + (z - sgn + NZ) % NZ
    sec_up = (sec + 1) % 8
    sec_dn = (sec + 7) % 8

    def at(block):
        return (block + 2 * NZ) % NZ

    def remote(src, dst, ss, rs, expert, section=None):
        return pltpu.make_async_remote_copy(
            src_ref=src, dst_ref=dst, send_sem=ss, recv_sem=rs,
            device_id=(sec if section is None else section, expert),
            device_id_type=pl.DeviceIdType.MESH)

    barrier = pltpu.get_barrier_semaphore()
    peers = [(sec, ((y + k) % NY) * NZ + z) for k in range(1, NY)]
    peers += [(sec, to_a), (sec, to_b), (sec_up, me), (sec_dn, me)]
    for peer in peers:
        pl.semaphore_signal(barrier, inc=1, device_id=peer, device_id_type=pl.DeviceIdType.MESH)

    def cols(half, c):
        return slice(half * W + c * C, half * W + (c + 1) * C)

    def own_rows(t, which, half, c):
        if t == 0:
            return (x_in, g_in)[which][:, cols(half, c)]
        return land[which, c, half]

    def pick(t, c):
        for half in range(2):
            here = cols(half, c)
            if t == 0:
                terms = (x_in[:, here], st_in[0, :, here], g_in[:, here], st_in[1, :, here])
                pk, pad, buf = pk0_in, PAD, sendy0
            else:
                terms = (land[0, c, half], land[1, c, half])
                pk, pad, buf = pk1_in, 8, sendy1
            picked = dot(pk[0], terms[0])
            for s in range(1, len(terms)):
                picked = picked + dot(pk[s], terms[s])
            picked = picked.astype(BF)
            for e in range(WINDOW):
                buf[2 * e + half, c] = picked[e * pad:(e + 1) * pad]

    def across(buf, got, ss, rs, t, c):
        copies = []
        for k in FAR_FIRST:
            to = (y + k) % NY
            copies.append(remote(buf.at[to, c], got.at[y, c], ss.at[t, c, k], rs.at[t, c, k], to * NZ + z))
        return copies

    def weight_copies():
        away = pl.ds(pl.multiple_of((1 - par) * W, 128), W)
        return (
            remote(up_in.at[1 - par], upf.at[par], w_ss.at[0], w_rs.at[0], mate),
            remote(dn_in.at[:, away], dnf.at[par], w_ss.at[1], w_rs.at[1], mate),
        )

    def shift_copies(c):
        return (
            remote(shout.at[0, c], land.at[0, c], s_ss.at[0, c], s_rs.at[0, c], me, sec_up),
            remote(shout.at[1, c], land.at[1, c], s_ss.at[1, c], s_rs.at[1, c], me, sec_dn),
        )

    def save_a(h):
        b = at(z - sgn * h)
        return remote(zsave.at[b], zsave.at[b], va_ss.at[h], va_rs.at[h], to_a)

    def save_b(h):
        b = at(z + sgn * h)
        return remote(zsave.at[b], zsave.at[b], vb_ss.at[h], vb_rs.at[h], to_b)

    def save_hop(h):
        save_a(h).wait_recv()
        if h < 3:
            save_a(h + 1).start()
            save_b(h).wait_recv()
            if h < 2:
                save_b(h + 1).start()

    for c in range(2):
        pick(0, c)
    pl.semaphore_wait(barrier, len(peers))

    started = []
    for t in range(STEPS):
        buf, got = ((sendy0, ybuf0), (sendy1, ybuf1))[t]
        zbuf = (zbuf0, zbuf1)[t]
        sent_y = []
        for c in range(2):
            if t == 1:
                for copy in shift_copies(c):
                    copy.wait_recv()

                @pl.when(sec == 0)
                def _():
                    for half in range(2):
                        land[0, c, half] = fx_in[:, cols(half, c)]

                @pl.when(sec == 7)
                def _():
                    for half in range(2):
                        land[1, c, half] = fg_in[:, cols(half, c)]

                pick(1, c)
            sent = across(buf, got, y_ss, y_rs, t, c)
            for copy in sent:
                copy.start()
            got[y, c] = buf[y, c]
            sent_y.append(sent)
        if t == 1:
            save_hop(2)

        def go_a(h, c):
            b = at(z - sgn * h)
            return remote(zbuf.at[b, c], zbuf.at[b, c], za_ss.at[t, h, c], za_rs.at[t, h, c], to_a)

        def go_b(h, c):
            b = at(z + sgn * h)
            return remote(zbuf.at[b, c], zbuf.at[b, c], zb_ss.at[t, h, c], zb_rs.at[t, h, c], to_b)

        def swap(b):
            return remote(xsend.at[t, b], xrecv.at[t, b], e_ss.at[t, b], e_rs.at[t, b], mate)

        for c in range(2):
            for copy in sent_y[c]:
                copy.wait_recv()
            if t == 0:
                gathered = dot(cmp0_in[...], got[:, c].reshape(NY * PAD, C)).astype(BF)
                zbuf[z, c] = gathered[:ROWS]
                zsave[z, :, c * C:(c + 1) * C] = gathered[ROWS:]
            else:
                stacked = got[:, c].astype(F32).reshape(NY * 8, C).astype(BF)
                zbuf[z, c] = dot(cmp1_in[...], stacked).astype(BF)
            go_a(0, c).start()
            go_b(0, c).start()
        if t == 0:
            for copy in weight_copies():
                copy.start()

            @pl.when(par == 0)
            def _():
                upf[0] = up_in[0]
                dnf[0] = dn_in[:, :W]

            @pl.when(par == 1)
            def _():
                upf[1] = up_in[1]
                dnf[1] = dn_in[:, W:]
        else:
            save_hop(3)

        def first_half(b):
            rows = [zbuf[b, c] for c in range(2)]
            if t == 0:
                pre = dot(rows[0][:BACK], upc[:C]) + dot(rows[1][:BACK], upc[C:])
                grads = [r[BACK:] for r in rows]
            else:
                wide = [r.astype(F32) for r in rows]
                ahead = [w[:HALF].astype(BF) for w in wide]
                grads = [w[HALF:].astype(BF) for w in wide]
                pre = jnp.concatenate([
                    dot(ahead[0], upc[:C]) + dot(ahead[1], upc[C:]),
                    dot(zsave[b], upc[...])], axis=0)
            down = dnf[...].reshape(2 * HID_DEV, W)
            dh = dot_t(grads[0], down[:, :C]) + dot_t(grads[1], down[:, C:])
            both = jnp.concatenate([pre, dh], axis=0)
            pp[t, b] = both
            xsend[t, b] = both.astype(BF)
            swap(b).start()

        if t == 1:
            first_half(z)
        for h in range(4):
            for c in range(2):
                go_a(h, c).wait_recv()
                if h < 3:
                    go_a(h + 1, c).start()
                    go_b(h, c).wait_recv()
                    if h < 2:
                        go_b(h + 1, c).start()
            fresh = [h]
            if t == 0:
                fresh = [[], [], [0, 1, 2], [3]][h]
                if h == 2:
                    for copy in weight_copies():
                        copy.wait()
                    upc[:, :HID_DEV] = upf[0]
                    upc[:, HID_DEV:] = upf[1]
                    first_half(z)
            for k in fresh:
                first_half(at(z - sgn * (k + 1)))
                if k < 3:
                    first_half(at(z + sgn * (k + 1)))

        def second_half(b):
            swap(b).wait_recv()
            both = pp[t, b] + xrecv[t, b].astype(F32)
            v = both[:HALF]
            hidden = (v / (1.0 + jnp.exp(-v))).astype(BF)
            u = both[HALF:BACK]
            sigma = 1.0 / (1.0 + jnp.exp(-u))
            dpre = (both[BACK:] * (sigma * (1.0 + u * (1.0 - sigma)))).astype(BF)
            part = dot(hidden, dnf[...].reshape(2 * HID_DEV, W))
            for c in range(2):
                dpart = dot_t(dpre, upc[c * C:(c + 1) * C])
                pbuf[t, b, c] = jnp.concatenate([part[:, c * C:(c + 1) * C], dpart], axis=0).astype(BF)

        def back_a(h, c):
            b = at(z + sgn * (4 - h))
            return remote(pbuf.at[t, b, c], ra.at[t, h, c], ra_ss.at[t, h, c], ra_rs.at[t, h, c], to_a)

        def back_b(h, c):
            b = at(z - sgn * (3 - h))
            return remote(pbuf.at[t, b, c], rb.at[t, h, c], rb_ss.at[t, h, c], rb_rs.at[t, h, c], to_b)

        for h in range(4):
            a = at(z + sgn * (4 - h))
            b = at(z - sgn * (3 - h))
            second_half(a)
            if h == 0:
                for c in range(2):
                    back_a(0, c).start()
            second_half(b)
            if h == 0:
                for c in range(2):
                    back_b(0, c).start()
                continue
            for c in range(2):
                back_a(h - 1, c).wait_recv()
                pbuf[t, a, c] = (pbuf[t, a, c].astype(F32) + ra[t, h - 1, c].astype(F32)).astype(BF)
                back_a(h, c).start()
                if h < 3:
                    back_b(h - 1, c).wait_recv()
                    pbuf[t, b, c] = (pbuf[t, b, c].astype(F32) + rb[t, h - 1, c].astype(F32)).astype(BF)
                    back_b(h, c).start()
        if t == 0:
            save_a(0).start()
            save_b(0).start()
        sent_t = []
        for c in range(2):
            back_b(2, c).wait_recv()
            back_a(3, c).wait_recv()
            total = (pbuf[t, z, c].astype(F32) + ra[t, 3, c].astype(F32) + rb[t, 2, c].astype(F32)).astype(BF)
            spread = dot(exp_in[...], total).astype(BF)
            for k in range(NY):
                rsend[t, k, c] = spread[k * 8:(k + 1) * 8]
            sent = across(rsend.at[t], ret.at[t], t_ss, t_rs, t, c)
            for copy in sent:
                copy.start()
            ret[t, y, c] = rsend[t, y, c]
            sent_t.append(sent)
        if t == 0:
            save_hop(0)
        for c in range(2):
            for copy in sent_t[c]:
                copy.wait_recv()
            for half in range(2):
                totals = jnp.concatenate([ret[t, 2 * e + half, c].astype(F32) for e in range(WINDOW)], axis=0)
                for which in range(2):
                    mixed = jnp.dot(sc_in[t, which], totals, precision=lax.Precision.HIGHEST,
                                    preferred_element_type=F32)
                    value = (own_rows(t, which, half, c).astype(F32) + mixed).astype(BF)
                    if t == 0:
                        shout[which, c, half] = value
                    else:
                        (out_ref, dx_ref)[which][:, cols(half, c)] = value
            if t == 0:
                for copy in shift_copies(c):
                    copy.start()
        if t == 0:
            save_hop(1)

        for c in range(2):
            started += sent_y[c] + sent_t[c]
            for h in range(4):
                started += [go_a(h, c), back_a(h, c)]
            for h in range(3):
                started += [go_b(h, c), back_b(h, c)]
            if t == 0:
                started += list(shift_copies(c))
        started += [swap(b) for b in range(NZ)]
    started += [save_a(h) for h in range(4)] + [save_b(h) for h in range(3)]
    for copy in started:
        copy.wait_send()


def slot_plan(routes, gates):
    match = routes[..., None] == jnp.arange(WINDOW, dtype=jnp.int32)
    chosen = jnp.sum(match.astype(F32), axis=2)
    weight = jnp.sum(jnp.where(match, gates[..., None], 0.0), axis=2)
    ranks = jnp.cumsum(chosen, axis=1) - chosen
    places = (ranks[..., None] == jnp.arange(CAP, dtype=F32)).astype(F32)
    return places * chosen[..., None], weight


def plans(fr, fg, br, bg):
    pf, wf = slot_plan(fr, fg)
    pb, wb = slot_plan(br, bg)

    def picker(places, s, pad):
        m = jnp.transpose(places, (1, 2, 0))
        m = jnp.pad(m, ((0, 0), (s * CAP, pad - (s + 1) * CAP), (0, 0)))
        return m.reshape(WINDOW * pad, TOK).astype(BF)

    def scaler(places, weight, s):
        m = places * weight[..., None]
        m = jnp.pad(m, ((0, 0), (0, 0), (0, 0), (s * CAP, 8 - (s + 1) * CAP)))
        return m.reshape(STEPS, TOK, WINDOW * 8)

    pick0 = jnp.stack([picker(p, s, PAD) for s, p in enumerate((pf[0], pb[0], pb[0], pb[1]))])
    pick1 = jnp.stack([picker(p, s, 8) for s, p in enumerate((pf[1], pb[1]))])
    scale = jnp.stack([scaler(pf, wf, 0), scaler(pb, wb, 1)], axis=1)
    return pick0, pick1, scale


def row_map(streams, pad, forward):
    i = np.arange(streams * HALF)
    j = np.arange(NY * pad)
    s, k, c = i // HALF, (i % HALF) // CAP, i % CAP
    hit = (k * pad + s * CAP + c)[:, None] == j[None, :]
    return jnp.asarray(hit if forward else hit.T, BF)


def local(activations, gradients, stashed, fresh_activations, fresh_gradients, w_up, w_down,
          forward_routes, forward_gates, backward_routes, backward_gates):
    pick0, pick1, scale = plans(forward_routes[:, 0], forward_gates[:, 0], backward_routes[:, 0], backward_gates[:, 0])
    up = w_up[0].reshape(2, W, HID_DEV)
    vmem = pl.BlockSpec(memory_space=pltpu.VMEM)
    dma = pltpu.SemaphoreType.DMA
    shape = jax.ShapeDtypeStruct((TOK, D), BF)
    S = STEPS
    out, dx = pl.pallas_call(
        kernel,
        out_shape=(shape, shape),
        in_specs=[vmem] * 13,
        out_specs=(vmem, vmem),
        scratch_shapes=[
            pltpu.VMEM((2, 2, 2, TOK, C), BF),
            pltpu.VMEM((2, 2, 2, TOK, C), BF),
            pltpu.VMEM((2, W, HID_DEV), BF),
            pltpu.VMEM((2, HID_DEV, W), BF),
            pltpu.VMEM((W, 2 * HID_DEV), BF),
            pltpu.VMEM((NY, 2, PAD, C), BF),
            pltpu.VMEM((NY, 2, PAD, C), BF),
            pltpu.VMEM((NY, 2, 8, C), BF),
            pltpu.VMEM((NY, 2, 8, C), BF),
            pltpu.VMEM((NZ, 2, ROWS, C), BF),
            pltpu.VMEM((NZ, 2, BACK, C), BF),
            pltpu.VMEM((NZ, HALF, W), BF),
            pltpu.VMEM((S, NZ, ROWS, 2 * HID_DEV), F32),
            pltpu.VMEM((S, NZ, ROWS, 2 * HID_DEV), BF),
            pltpu.VMEM((S, NZ, ROWS, 2 * HID_DEV), BF),
            pltpu.VMEM((S, NZ, 2, BACK, C), BF),
            pltpu.VMEM((S, 4, 2, BACK, C), BF),
            pltpu.VMEM((S, 3, 2, BACK, C), BF),
            pltpu.VMEM((S, NY, 2, 8, C), BF),
            pltpu.VMEM((S, NY, 2, 8, C), BF),
            dma((2,)), dma((2,)),
            dma((S, 2, NY)), dma((S, 2, NY)),
            dma((S, 4, 2)), dma((S, 4, 2)),
            dma((S, 3, 2)), dma((S, 3, 2)),
            dma((4,)), dma((4,)),
            dma((3,)), dma((3,)),
            dma((S, NZ)), dma((S, NZ)),
            dma((S, 4, 2)), dma((S, 4, 2)),
            dma((S, 3, 2)), dma((S, 3, 2)),
            dma((S, 2, NY)), dma((S, 2, NY)),
            dma((2, 2)), dma((2, 2)),
        ],
        compiler_params=pltpu.CompilerParams(
            collective_id=0, has_side_effects=True, vmem_limit_bytes=60 * 1024 * 1024),
    )(activations[0], gradients[0], stashed[:, 0], fresh_activations[0], fresh_gradients[0],
      up, w_down[0], pick0, pick1, scale, row_map(4, PAD, True), row_map(2, 8, True), row_map(2, 8, False))
    return out[None], dx[None]


def solution(mesh):
    placed = (
        P("section", "expert", None),
        P("section", "expert", None),
        P(None, "section", "expert", None),
        P(None, "expert", None),
        P(None, "expert", None),
        P("section", None, "expert"),
        P("section", "expert", None),
        P(None, "section", "expert", None),
        P(None, "section", "expert", None),
        P(None, "section", "expert", None),
        P(None, "section", "expert", None),
    )
    return jax.shard_map(
        local,
        mesh=mesh,
        in_specs=placed,
        out_specs=(P("section", "expert", None), P("section", "expert", None)),
        check_vma=False,
    )
```

time: 174 us -> 147 us (0.84)
  Pallas kernels: 164 us -> 139 us
    pallas_call x1, Pallas kernels: 164 us -> 139 us  [local(): pl.pallas_call(kernel, out_shape=(shape, shape), in_specs=[vmem] * 13, ou...]
    unnamed x14 -> x12, local copies, waits for them, and re-layouts: 4.02 us -> 4.02 us
where the time goes in v2:
time: 147 us; the launch traced here: 146 us
  Pallas kernels  139 us (95%)
  local copies, waits for them, and re-layouts  4.62 us (3%)
  other arithmetic  2.26 us (2%)
    pallas_call x1, Pallas kernels, local(): pl.pallas_call(kernel, out_shape=(shape, shape), in_specs=[vmem] * 13, ou...  139 us
    unnamed x12, local copies, waits for them, and re-layouts  4.02 us

profile of v2, /device:TPU:6, one launch (start us, length us, event | category | flops | bytes accessed | tf_op | source)
XLA Modules:
  0.0 146.5 jit_solution(11960359867640396767)
XLA Ops:
  0.6 0.0 copy-start.2
  0.6 0.0 copy-start.1
  0.7 0.7 copy-done.2
  1.3 0.0 copy-done.1
  1.3 0.0 copy-start.3
  1.3 0.0 copy-start.4
  1.4 0.7 copy-done.3
  2.0 0.0 copy-done.4
  2.1 0.1 copy.39
  2.2 0.1 copy.36
  2.3 0.1 reduce_window_sum.17
  2.4 0.1 copy.38
  2.6 0.1 copy.42
  2.7 0.1 reduce_window_sum.18
  2.8 0.1 copy.41
  3.0 0.6 pad_maximum_fusion.2.pk1_in
  3.6 0.7 pad_maximum_fusion.1.pk0_in
  4.3 0.1 copy.43
  4.3 0.7 pad_maximum_fusion.sc_in
  5.0 138.8 %shard_map.149 = (bf16[64,3584]{1,0:T(8,128)(2,1)}, bf16[64,3584]{1,0:T(8,128)(2,1)}) custom-call(bf16[64,3584]{1,0:T(8,128)(2,1)} %bitcast.46, bf16[64,3584]{1,0:T(8,128)(2,1)} %bitcast.47, bf16[2,64,3584]{2,1,0:T(8,128)(2,1)} %bitcast.41, bf16[64,3584]{1,0:T(8,128)(2,1)} %bitcast.48, bf16[64,3584]{1,0:T(8,128)(2,1)} %bitcast.49, ...), custom_call_target="tpu_custom_call" | custom-call | tf_op jit(solution)/shard_map/pallas_call | solution.py:383
  143.8 0.0 copy-start
  143.8 1.9 %copy.46 = bf16[1,64,3584]{2,1,0:T(8,128)(2,1)} copy(bf16[1,64,3584]{2,1,0:T(8,128)(2,1)} %bitcast.45) | data formatting | bytes 917504
  145.7 0.0 copy-done
  145.7 0.8 copy.47
  (16 shorter events, 0.2 us)
Async XLA Ops:
  0.6 0.7 copy-start.2
  0.6 0.7 copy-start.1
  1.3 0.7 copy-start.3
  1.3 0.7 copy-start.4
  143.8 1.9 %copy-start = (bf16[64,3584]{1,0:T(8,128)(2,1)S(1)}, bf16[64,3584]{1,0:T(8,128)(2,1)}, u32[]{:S(2)}) copy-start(bf16[64,3584]{1,0:T(8,128)(2,1)} %get-tuple-element.5) | copy-start | bytes 1376260

commit v3 on v2

--- a/solution.py
+++ b/solution.py
@@ -34,12 +34,13 @@
     return lax.dot_general(a, b, TRANS, preferred_element_type=F32)
 
 
-def kernel(x_in, g_in, st_in, fx_in, fg_in, up_in, dn_in, pk0_in, pk1_in, sc_in, cmp0_in, cmp1_in, exp_in,
+def kernel(x_in, g_in, st_in, fx_in, fg_in, up_in, dn_in, fr_in, fg_w, br_in, bg_w, cmp0_in, cmp1_in, exp_in,
            out_ref, dx_ref,
            shout, land, upf, dnf, upc, sendy0, ybuf0, sendy1, ybuf1, zbuf0, zbuf1, zsave, pp, xsend, xrecv,
            pbuf, ra, rb, rsend, ret,
            w_ss, w_rs, y_ss, y_rs, za_ss, za_rs, zb_ss, zb_rs, va_ss, va_rs, vb_ss, vb_rs, e_ss, e_rs,
-           ra_ss, ra_rs, rb_ss, rb_rs, t_ss, t_rs, s_ss, s_rs):
+           ra_ss, ra_rs, rb_ss, rb_rs, t_ss, t_rs, s_ss, s_rs, d_ss, d_rs,
+           dsend, drecv, pk0, pk1, scales):
     sec = lax.axis_index("section")
     me = lax.axis_index("expert")
     y = me // NZ
@@ -81,10 +82,10 @@
             here = cols(half, c)
             if t == 0:
                 terms = (x_in[:, here], st_in[0, :, here], g_in[:, here], st_in[1, :, here])
-                pk, pad, buf = pk0_in, PAD, sendy0
+                pk, pad, buf = pk0, PAD, sendy0
             else:
                 terms = (land[0, c, half], land[1, c, half])
-                pk, pad, buf = pk1_in, 8, sendy1
+                pk, pad, buf = pk1, 8, sendy1
             picked = dot(pk[0], terms[0])
             for s in range(1, len(terms)):
                 picked = picked + dot(pk[s], terms[s])
@@ -127,6 +128,44 @@
             save_b(h).wait_recv()
             if h < 2:
                 save_b(h + 1).start()
+
+    earlier = (lax.broadcasted_iota(jnp.int32, (TOK, TOK), 1)
+               < lax.broadcasted_iota(jnp.int32, (TOK, TOK), 0)).astype(F32).astype(BF)
+    wide = lax.broadcasted_iota(jnp.int32, (TOK, WINDOW * PAD), 1)
+    thin = lax.broadcasted_iota(jnp.int32, (TOK, WINDOW * 8), 1)
+    for t in range(STEPS):
+        for which, (routes, gates) in enumerate(((fr_in, fg_w), (br_in, bg_w))):
+            ids, weights = routes[t], gates[t]
+            named, weight = [], []
+            for e in range(WINDOW):
+                match = ids == e
+                named.append(jnp.sum(jnp.where(match, 1.0, 0.0), axis=1, keepdims=True))
+                weight.append(jnp.sum(jnp.where(match, weights, 0.0), axis=1, keepdims=True))
+            scaled = jnp.zeros((TOK, WINDOW * 8), F32)
+            places = [jnp.zeros((TOK, WINDOW * PAD), F32) for s in range(4)]
+            short = jnp.zeros((TOK, WINDOW * 8), F32)
+            for e in range(WINDOW):
+                rank = dot(earlier, jnp.broadcast_to(named[e], (TOK, 128)).astype(BF))[:, :1]
+                for c in range(CAP):
+                    here = jnp.where(rank == float(c), named[e], 0.0)
+                    scaled = scaled + jnp.where(thin == e * 8 + which * CAP + c, here * weight[e], 0.0)
+                    short = short + jnp.where(thin == e * 8 + which * CAP + c, here, 0.0)
+                    for s in range(4):
+                        places[s] = places[s] + jnp.where(wide == e * PAD + s * CAP + c, here, 0.0)
+            high = scaled.astype(BF)
+            left = scaled - high.astype(F32)
+            mid = left.astype(BF)
+            low = (left - mid.astype(F32)).astype(BF)
+            scales[t, which, 0] = high
+            scales[t, which, 1] = mid
+            scales[t, which, 2] = low
+            if t == 0:
+                for s in ((0,), (1, 2))[which]:
+                    pk0[s] = places[s].T.astype(BF)
+            else:
+                pk1[which] = short.T.astype(BF)
+                if which == 1:
+                    pk0[3] = places[3].T.astype(BF)
 
     for c in range(2):
         pick(0, c)
@@ -172,6 +211,9 @@
         def swap(b):
             return remote(xsend.at[t, b], xrecv.at[t, b], e_ss.at[t, b], e_rs.at[t, b], mate)
 
+        def swap_d(b):
+            return remote(dsend.at[t, b], drecv.at[t, b], d_ss.at[t, b], d_rs.at[t, b], mate)
+
         for c in range(2):
             for copy in sent_y[c]:
                 copy.wait_recv()
@@ -184,10 +226,10 @@
                 zbuf[z, c] = dot(cmp1_in[...], stacked).astype(BF)
             go_a(0, c).start()
             go_b(0, c).start()
+            if t == 0 and c == 0:
+                for copy in weight_copies():
+                    copy.start()
         if t == 0:
-            for copy in weight_copies():
-                copy.start()
-
             @pl.when(par == 0)
             def _():
                 upf[0] = up_in[0]
@@ -200,27 +242,37 @@
         else:
             save_hop(3)
 
-        def first_half(b):
+        def pre_half(b):
             rows = [zbuf[b, c] for c in range(2)]
             if t == 0:
                 pre = dot(rows[0][:BACK], upc[:C]) + dot(rows[1][:BACK], upc[C:])
-                grads = [r[BACK:] for r in rows]
             else:
-                wide = [r.astype(F32) for r in rows]
-                ahead = [w[:HALF].astype(BF) for w in wide]
-                grads = [w[HALF:].astype(BF) for w in wide]
+                ahead = [r.astype(F32)[:HALF].astype(BF) for r in rows]
                 pre = jnp.concatenate([
                     dot(ahead[0], upc[:C]) + dot(ahead[1], upc[C:]),
                     dot(zsave[b], upc[...])], axis=0)
+            pp[t, b, :BACK] = pre
+            xsend[t, b] = pre.astype(BF)
+            swap(b).start()
+
+        def grad_half(b):
+            rows = [zbuf[b, c] for c in range(2)]
+            if t == 0:
+                grads = [r[BACK:] for r in rows]
+            else:
+                grads = [r.astype(F32)[HALF:].astype(BF) for r in rows]
             down = dnf[...].reshape(2 * HID_DEV, W)
             dh = dot_t(grads[0], down[:, :C]) + dot_t(grads[1], down[:, C:])
-            both = jnp.concatenate([pre, dh], axis=0)
-            pp[t, b] = both
-            xsend[t, b] = both.astype(BF)
-            swap(b).start()
+            pp[t, b, BACK:] = dh
+            dsend[t, b] = dh.astype(BF)
+            swap_d(b).start()
+
+        def landed(k):
+            return [at(z - sgn * (k + 1))] + ([at(z + sgn * (k + 1))] if k < 3 else [])
 
         if t == 1:
-            first_half(z)
+            pre_half(z)
+            grad_half(z)
         for h in range(4):
             for c in range(2):
                 go_a(h, c).wait_recv()
@@ -229,28 +281,33 @@
                     go_b(h, c).wait_recv()
                     if h < 2:
                         go_b(h + 1, c).start()
-            fresh = [h]
-            if t == 0:
-                fresh = [[], [], [0, 1, 2], [3]][h]
-                if h == 2:
-                    for copy in weight_copies():
-                        copy.wait()
-                    upc[:, :HID_DEV] = upf[0]
-                    upc[:, HID_DEV:] = upf[1]
-                    first_half(z)
-            for k in fresh:
-                first_half(at(z - sgn * (k + 1)))
-                if k < 3:
-                    first_half(at(z + sgn * (k + 1)))
+            if t == 0 and h == 1:
+                weight_copies()[0].wait()
+                upc[:, :HID_DEV] = upf[0]
+                upc[:, HID_DEV:] = upf[1]
+                for b in [z] + landed(0):
+                    pre_half(b)
+            if t == 1 or h >= 1:
+                for b in landed(h):
+                    pre_half(b)
+            if t == 0 and h == 2:
+                weight_copies()[1].wait()
+                for b in [z] + landed(0) + landed(1):
+                    grad_half(b)
+            if t == 1 or h >= 2:
+                for b in landed(h):
+                    grad_half(b)
 
         def second_half(b):
             swap(b).wait_recv()
-            both = pp[t, b] + xrecv[t, b].astype(F32)
+            both = pp[t, b, :BACK] + xrecv[t, b].astype(F32)
             v = both[:HALF]
             hidden = (v / (1.0 + jnp.exp(-v))).astype(BF)
             u = both[HALF:BACK]
             sigma = 1.0 / (1.0 + jnp.exp(-u))
-            dpre = (both[BACK:] * (sigma * (1.0 + u * (1.0 - sigma)))).astype(BF)
+            swap_d(b).wait_recv()
+            slope_in = pp[t, b, BACK:] + drecv[t, b].astype(F32)
+            dpre = (slope_in * (sigma * (1.0 + u * (1.0 - sigma)))).astype(BF)
             part = dot(hidden, dnf[...].reshape(2 * HID_DEV, W))
             for c in range(2):
                 dpart = dot_t(dpre, upc[c * C:(c + 1) * C])
@@ -306,10 +363,10 @@
             for copy in sent_t[c]:
                 copy.wait_recv()
             for half in range(2):
-                totals = jnp.concatenate([ret[t, 2 * e + half, c].astype(F32) for e in range(WINDOW)], axis=0)
+                totals = jnp.concatenate([ret[t, 2 * e + half, c].astype(F32) for e in range(WINDOW)], axis=0).astype(BF)
                 for which in range(2):
-                    mixed = jnp.dot(sc_in[t, which], totals, precision=lax.Precision.HIGHEST,
-                                    preferred_element_type=F32)
+                    mixed = (dot(scales[t, which, 2], totals) + dot(scales[t, which, 1], totals)
+                             + dot(scales[t, which, 0], totals))
                     value = (own_rows(t, which, half, c).astype(F32) + mixed).astype(BF)
                     if t == 0:
                         shout[which, c, half] = value
@@ -329,39 +386,10 @@
                 started += [go_b(h, c), back_b(h, c)]
             if t == 0:
                 started += list(shift_copies(c))
-        started += [swap(b) for b in range(NZ)]
+        started += [swap(b) for b in range(NZ)] + [swap_d(b) for b in range(NZ)]
     started += [save_a(h) for h in range(4)] + [save_b(h) for h in range(3)]
     for copy in started:
         copy.wait_send()
-
-
-def slot_plan(routes, gates):
-    match = routes[..., None] == jnp.arange(WINDOW, dtype=jnp.int32)
-    chosen = jnp.sum(match.astype(F32), axis=2)
-    weight = jnp.sum(jnp.where(match, gates[..., None], 0.0), axis=2)
-    ranks = jnp.cumsum(chosen, axis=1) - chosen
-    places = (ranks[..., None] == jnp.arange(CAP, dtype=F32)).astype(F32)
-    return places * chosen[..., None], weight
-
-
-def plans(fr, fg, br, bg):
-    pf, wf = slot_plan(fr, fg)
-    pb, wb = slot_plan(br, bg)
-
-    def picker(places, s, pad):
-        m = jnp.transpose(places, (1, 2, 0))
-        m = jnp.pad(m, ((0, 0), (s * CAP, pad - (s + 1) * CAP), (0, 0)))
-        return m.reshape(WINDOW * pad, TOK).astype(BF)
-
-    def scaler(places, weight, s):
-        m = places * weight[..., None]
-        m = jnp.pad(m, ((0, 0), (0, 0), (0, 0), (s * CAP, 8 - (s + 1) * CAP)))
-        return m.reshape(STEPS, TOK, WINDOW * 8)
-
-    pick0 = jnp.stack([picker(p, s, PAD) for s, p in enumerate((pf[0], pb[0], pb[0], pb[1]))])
-    pick1 = jnp.stack([picker(p, s, 8) for s, p in enumerate((pf[1], pb[1]))])
-    scale = jnp.stack([scaler(pf, wf, 0), scaler(pb, wb, 1)], axis=1)
-    return pick0, pick1, scale
 
 
 def row_map(streams, pad, forward):
@@ -374,7 +402,6 @@
 
 def local(activations, gradients, stashed, fresh_activations, fresh_gradients, w_up, w_down,
           forward_routes, forward_gates, backward_routes, backward_gates):
-    pick0, pick1, scale = plans(forward_routes[:, 0], forward_gates[:, 0], backward_routes[:, 0], backward_gates[:, 0])
     up = w_up[0].reshape(2, W, HID_DEV)
     vmem = pl.BlockSpec(memory_space=pltpu.VMEM)
     dma = pltpu.SemaphoreType.DMA
@@ -383,7 +410,7 @@
     out, dx = pl.pallas_call(
         kernel,
         out_shape=(shape, shape),
-        in_specs=[vmem] * 13,
+        in_specs=[vmem] * 14,
         out_specs=(vmem, vmem),
         scratch_shapes=[
             pltpu.VMEM((2, 2, 2, TOK, C), BF),
@@ -399,8 +426,8 @@
             pltpu.VMEM((NZ, 2, BACK, C), BF),
             pltpu.VMEM((NZ, HALF, W), BF),
             pltpu.VMEM((S, NZ, ROWS, 2 * HID_DEV), F32),
-            pltpu.VMEM((S, NZ, ROWS, 2 * HID_DEV), BF),
-            pltpu.VMEM((S, NZ, ROWS, 2 * HID_DEV), BF),
+            pltpu.VMEM((S, NZ, BACK, 2 * HID_DEV), BF),
+            pltpu.VMEM((S, NZ, BACK, 2 * HID_DEV), BF),
             pltpu.VMEM((S, NZ, 2, BACK, C), BF),
             pltpu.VMEM((S, 4, 2, BACK, C), BF),
             pltpu.VMEM((S, 3, 2, BACK, C), BF),
@@ -417,11 +444,19 @@
             dma((S, 3, 2)), dma((S, 3, 2)),
             dma((S, 2, NY)), dma((S, 2, NY)),
             dma((2, 2)), dma((2, 2)),
+            dma((S, NZ)), dma((S, NZ)),
+            pltpu.VMEM((S, NZ, HALF, 2 * HID_DEV), BF),
+            pltpu.VMEM((S, NZ, HALF, 2 * HID_DEV), BF),
+            pltpu.VMEM((4, WINDOW * PAD, TOK), BF),
+            pltpu.VMEM((2, WINDOW * 8, TOK), BF),
+            pltpu.VMEM((S, 2, 3, TOK, WINDOW * 8), BF),
         ],
         compiler_params=pltpu.CompilerParams(
             collective_id=0, has_side_effects=True, vmem_limit_bytes=60 * 1024 * 1024),
     )(activations[0], gradients[0], stashed[:, 0], fresh_activations[0], fresh_gradients[0],
-      up, w_down[0], pick0, pick1, scale, row_map(4, PAD, True), row_map(2, 8, True), row_map(2, 8, False))
+      up, w_down[0], forward_routes[:, 0], forward_gates[:, 0],
+      backward_routes[:, 0], backward_gates[:, 0],
+      row_map(4, PAD, True), row_map(2, 8, True), row_map(2, 8, False))
     return out[None], dx[None]
 
 

time: 147 us -> 143 us (0.973)
  Pallas kernels: 139 us -> 136 us
  other arithmetic: 2.26 us -> 0 us
  local copies, waits for them, and re-layouts: 4.62 us -> 6.24 us
    pallas_call x1, Pallas kernels: 139 us -> 136 us  [local(): pl.pallas_call(kernel, out_shape=(shape, shape), in_specs=[vmem] * 14, ou...]
    unnamed x12 -> x16, local copies, waits for them, and re-layouts: 4.02 us -> 6.24 us
    another operation x6 -> x0, other arithmetic: 2.14 us -> none  [the longest x1 0.67 us: plans(): scale = jnp.stack([scaler(pf, wf, 0), scaler(pb, wb, 1)], axis=1)]
where the time goes in v3:
time: 143 us; the launch traced here: 142 us
  Pallas kernels  136 us (95%)
  local copies, waits for them, and re-layouts  6.24 us (4%)
    pallas_call x1, Pallas kernels, local(): pl.pallas_call(kernel, out_shape=(shape, shape), in_specs=[vmem] * 14, ou...  136 us
    unnamed x16, local copies, waits for them, and re-layouts  6.24 us

profile of v3, /device:TPU:6, one launch (start us, length us, event | category | flops | bytes accessed | tf_op | source)
XLA Modules:
  0.0 142.4 jit_solution(4228653795188235303)
XLA Ops:
  0.6 0.0 copy-start.1
  0.6 0.7 copy-done.1
  1.3 0.0 copy-start.2
  1.3 0.7 copy.16
  2.1 0.0 copy-done.2
  2.1 0.0 copy-start.3
  2.1 0.7 copy.17
  2.8 0.0 copy-done.3
  2.8 0.0 copy-start.4
  2.8 0.7 copy.18
  3.5 0.0 copy-done.4
  3.5 0.7 copy.19
  4.2 135.5 %shard_map.149 = (bf16[64,3584]{1,0:T(8,128)(2,1)}, bf16[64,3584]{1,0:T(8,128)(2,1)}) custom-call(bf16[64,3584]{1,0:T(8,128)(2,1)} %bitcast.18, bf16[64,3584]{1,0:T(8,128)(2,1)} %bitcast.19, bf16[2,64,3584]{2,1,0:T(8,128)(2,1)} %bitcast.13, bf16[64,3584]{1,0:T(8,128)(2,1)} %bitcast.20, bf16[64,3584]{1,0:T(8,128)(2,1)} %bitcast.21, ...), custom_call_target="tpu_custom_call" | custom-call | tf_op jit(solution)/shard_map/pallas_call | solution.py:410
  139.8 0.0 copy-start
  139.8 1.9 %copy.22 = bf16[1,64,3584]{2,1,0:T(8,128)(2,1)} copy(bf16[1,64,3584]{2,1,0:T(8,128)(2,1)} %bitcast.17) | data formatting | bytes 917504
  141.7 0.0 copy-done
  141.7 0.8 copy.23
Async XLA Ops:
  0.6 0.7 copy-start.1
  1.3 0.7 copy-start.2
  2.1 0.7 copy-start.3
  2.8 0.7 copy-start.4
  139.8 1.9 %copy-start = (bf16[64,3584]{1,0:T(8,128)(2,1)S(1)}, bf16[64,3584]{1,0:T(8,128)(2,1)}, u32[]{:S(2)}) copy-start(bf16[64,3584]{1,0:T(8,128)(2,1)} %get-tuple-element.5) | copy-start | bytes 1376260

commit v4 on v3

--- a/solution.py
+++ b/solution.py
@@ -40,7 +40,7 @@
            pbuf, ra, rb, rsend, ret,
            w_ss, w_rs, y_ss, y_rs, za_ss, za_rs, zb_ss, zb_rs, va_ss, va_rs, vb_ss, vb_rs, e_ss, e_rs,
            ra_ss, ra_rs, rb_ss, rb_rs, t_ss, t_rs, s_ss, s_rs, d_ss, d_rs,
-           dsend, drecv, pk0, pk1, scales):
+           dsend, drecv, pk0, pk1, scales, l_sem):
     sec = lax.axis_index("section")
     me = lax.axis_index("expert")
     y = me // NZ
@@ -107,6 +107,13 @@
             remote(dn_in.at[:, away], dnf.at[par], w_ss.at[1], w_rs.at[1], mate),
         )
 
+    def own_weights():
+        mine = pl.ds(pl.multiple_of(par * W, 128), W)
+        return (
+            pltpu.make_async_copy(up_in.at[par], upf.at[par], l_sem.at[0]),
+            pltpu.make_async_copy(dn_in.at[:, mine], dnf.at[par], l_sem.at[1]),
+        )
+
     def shift_copies(c):
         return (
             remote(shout.at[0, c], land.at[0, c], s_ss.at[0, c], s_rs.at[0, c], me, sec_up),
@@ -129,29 +136,32 @@
             if h < 2:
                 save_b(h + 1).start()
 
-    earlier = (lax.broadcasted_iota(jnp.int32, (TOK, TOK), 1)
-               < lax.broadcasted_iota(jnp.int32, (TOK, TOK), 0)).astype(F32).astype(BF)
-    wide = lax.broadcasted_iota(jnp.int32, (TOK, WINDOW * PAD), 1)
-    thin = lax.broadcasted_iota(jnp.int32, (TOK, WINDOW * 8), 1)
+    for copy in own_weights():
+        copy.start()
+    earlier = (lax.broadcasted_iota(jnp.int32, (TOK, TOK), 0)
+               < lax.broadcasted_iota(jnp.int32, (TOK, TOK), 1)).astype(F32).astype(BF)
+    wide = lax.broadcasted_iota(jnp.int32, (WINDOW * PAD, TOK), 0)
+    thin = lax.broadcasted_iota(jnp.int32, (WINDOW * 8, TOK), 0)
     for t in range(STEPS):
         for which, (routes, gates) in enumerate(((fr_in, fg_w), (br_in, bg_w))):
             ids, weights = routes[t], gates[t]
             named, weight = [], []
             for e in range(WINDOW):
                 match = ids == e
-                named.append(jnp.sum(jnp.where(match, 1.0, 0.0), axis=1, keepdims=True))
-                weight.append(jnp.sum(jnp.where(match, weights, 0.0), axis=1, keepdims=True))
-            scaled = jnp.zeros((TOK, WINDOW * 8), F32)
-            places = [jnp.zeros((TOK, WINDOW * PAD), F32) for s in range(4)]
-            short = jnp.zeros((TOK, WINDOW * 8), F32)
+                named.append(jnp.sum(jnp.where(match, 1.0, 0.0), axis=0, keepdims=True))
+                weight.append(jnp.sum(jnp.where(match, weights, 0.0), axis=0, keepdims=True))
+            scaled = jnp.zeros((WINDOW * 8, TOK), F32)
+            places = [jnp.zeros((WINDOW * PAD, TOK), F32) for s in range(4)]
+            short = jnp.zeros((WINDOW * 8, TOK), F32)
             for e in range(WINDOW):
-                rank = dot(earlier, jnp.broadcast_to(named[e], (TOK, 128)).astype(BF))[:, :1]
+                rank = dot(jnp.broadcast_to(named[e], (16, TOK)).astype(BF), earlier)[:1]
                 for c in range(CAP):
                     here = jnp.where(rank == float(c), named[e], 0.0)
                     scaled = scaled + jnp.where(thin == e * 8 + which * CAP + c, here * weight[e], 0.0)
                     short = short + jnp.where(thin == e * 8 + which * CAP + c, here, 0.0)
                     for s in range(4):
                         places[s] = places[s] + jnp.where(wide == e * PAD + s * CAP + c, here, 0.0)
+            scaled = scaled.T
             high = scaled.astype(BF)
             left = scaled - high.astype(F32)
             mid = left.astype(BF)
@@ -161,11 +171,11 @@
             scales[t, which, 2] = low
             if t == 0:
                 for s in ((0,), (1, 2))[which]:
-                    pk0[s] = places[s].T.astype(BF)
+                    pk0[s] = places[s].astype(BF)
             else:
-                pk1[which] = short.T.astype(BF)
+                pk1[which] = short.astype(BF)
                 if which == 1:
-                    pk0[3] = places[3].T.astype(BF)
+                    pk0[3] = places[3].astype(BF)
 
     for c in range(2):
         pick(0, c)
@@ -229,17 +239,7 @@
             if t == 0 and c == 0:
                 for copy in weight_copies():
                     copy.start()
-        if t == 0:
-            @pl.when(par == 0)
-            def _():
-                upf[0] = up_in[0]
-                dnf[0] = dn_in[:, :W]
-
-            @pl.when(par == 1)
-            def _():
-                upf[1] = up_in[1]
-                dnf[1] = dn_in[:, W:]
-        else:
+        if t == 1:
             save_hop(3)
 
         def pre_half(b):
@@ -269,34 +269,6 @@
 
         def landed(k):
             return [at(z - sgn * (k + 1))] + ([at(z + sgn * (k + 1))] if k < 3 else [])
-
-        if t == 1:
-            pre_half(z)
-            grad_half(z)
-        for h in range(4):
-            for c in range(2):
-                go_a(h, c).wait_recv()
-                if h < 3:
-                    go_a(h + 1, c).start()
-                    go_b(h, c).wait_recv()
-                    if h < 2:
-                        go_b(h + 1, c).start()
-            if t == 0 and h == 1:
-                weight_copies()[0].wait()
-                upc[:, :HID_DEV] = upf[0]
-                upc[:, HID_DEV:] = upf[1]
-                for b in [z] + landed(0):
-                    pre_half(b)
-            if t == 1 or h >= 1:
-                for b in landed(h):
-                    pre_half(b)
-            if t == 0 and h == 2:
-                weight_copies()[1].wait()
-                for b in [z] + landed(0) + landed(1):
-                    grad_half(b)
-            if t == 1 or h >= 2:
-                for b in landed(h):
-                    grad_half(b)
 
         def second_half(b):
             swap(b).wait_recv()
@@ -321,6 +293,41 @@
             b = at(z - sgn * (3 - h))
             return remote(pbuf.at[t, b, c], rb.at[t, h, c], rb_ss.at[t, h, c], rb_rs.at[t, h, c], to_b)
 
+        if t == 1:
+            pre_half(z)
+            grad_half(z)
+        for h in range(4):
+            for c in range(2):
+                go_a(h, c).wait_recv()
+                if h < 3:
+                    go_a(h + 1, c).start()
+                    go_b(h, c).wait_recv()
+                    if h < 2:
+                        go_b(h + 1, c).start()
+            if t == 0 and h == 1:
+                weight_copies()[0].wait()
+                own_weights()[0].wait()
+                upc[:, :HID_DEV] = upf[0]
+                upc[:, HID_DEV:] = upf[1]
+                for b in [z] + landed(0):
+                    pre_half(b)
+            if t == 1 or h >= 1:
+                for b in landed(h):
+                    pre_half(b)
+            if t == 0 and h == 2:
+                weight_copies()[1].wait()
+                own_weights()[1].wait()
+                for b in [z] + landed(0) + landed(1):
+                    grad_half(b)
+            if t == 1 or h >= 2:
+                for b in landed(h):
+                    grad_half(b)
+            if h == 2:
+                first_b = at(z - sgn * 3)
+                second_half(first_b)
+                for c in range(2):
+                    back_b(0, c).start()
+
         for h in range(4):
             a = at(z + sgn * (4 - h))
             b = at(z - sgn * (3 - h))
@@ -328,11 +335,8 @@
             if h == 0:
                 for c in range(2):
                     back_a(0, c).start()
+                continue
             second_half(b)
-            if h == 0:
-                for c in range(2):
-                    back_b(0, c).start()
-                continue
             for c in range(2):
                 back_a(h - 1, c).wait_recv()
                 pbuf[t, a, c] = (pbuf[t, a, c].astype(F32) + ra[t, h - 1, c].astype(F32)).astype(BF)
@@ -410,7 +414,7 @@
     out, dx = pl.pallas_call(
         kernel,
         out_shape=(shape, shape),
-        in_specs=[vmem] * 14,
+        in_specs=[vmem] * 5 + [pl.BlockSpec(memory_space=pl.ANY)] * 2 + [vmem] * 7,
         out_specs=(vmem, vmem),
         scratch_shapes=[
             pltpu.VMEM((2, 2, 2, TOK, C), BF),
@@ -450,12 +454,13 @@
             pltpu.VMEM((4, WINDOW * PAD, TOK), BF),
             pltpu.VMEM((2, WINDOW * 8, TOK), BF),
             pltpu.VMEM((S, 2, 3, TOK, WINDOW * 8), BF),
+            dma((2,)),
         ],
         compiler_params=pltpu.CompilerParams(
             collective_id=0, has_side_effects=True, vmem_limit_bytes=60 * 1024 * 1024),
     )(activations[0], gradients[0], stashed[:, 0], fresh_activations[0], fresh_gradients[0],
-      up, w_down[0], forward_routes[:, 0], forward_gates[:, 0],
-      backward_routes[:, 0], backward_gates[:, 0],
+      up, w_down[0], jnp.swapaxes(forward_routes[:, 0], 1, 2), jnp.swapaxes(forward_gates[:, 0], 1, 2),
+      jnp.swapaxes(backward_routes[:, 0], 1, 2), jnp.swapaxes(backward_gates[:, 0], 1, 2),
       row_map(4, PAD, True), row_map(2, 8, True), row_map(2, 8, False))
     return out[None], dx[None]
 

time: 143 us -> 142 us (level)
  local copies, waits for them, and re-layouts: 6.24 us -> 2.64 us
  Pallas kernels: 136 us -> 139 us
    unnamed x16 -> x4, local copies, waits for them, and re-layouts: 6.24 us -> 2.64 us
    pallas_call x1, Pallas kernels: 136 us -> 139 us  [local(): pl.pallas_call(kernel, out_shape=(shape, shape), in_specs=[vmem] * 5 + [p...]
where the time goes in v4:
time: 142 us
  Pallas kernels  139 us (98%)
  local copies, waits for them, and re-layouts  2.64 us (2%)
    pallas_call x1, Pallas kernels, local(): pl.pallas_call(kernel, out_shape=(shape, shape), in_specs=[vmem] * 5 + [p...  139 us

profile of v4, /device:TPU:6, one launch (start us, length us, event | category | flops | bytes accessed | tf_op | source)
XLA Modules:
  0.0 141.9 jit_solution(6816789929820026125)
XLA Ops:
  0.6 138.6 %shard_map.149 = (bf16[64,3584]{1,0:T(8,128)(2,1)}, bf16[64,3584]{1,0:T(8,128)(2,1)}) custom-call(bf16[64,3584]{1,0:T(8,128)(2,1)} %bitcast.26, bf16[64,3584]{1,0:T(8,128)(2,1)} %bitcast.27, bf16[2,64,3584]{2,1,0:T(8,128)(2,1)} %bitcast.21, bf16[64,3584]{1,0:T(8,128)(2,1)} %bitcast.28, bf16[64,3584]{1,0:T(8,128)(2,1)} %bitcast.29, ...), custom_call_target="tpu_custom_call" | custom-call | tf_op jit(solution)/shard_map/pallas_call | solution.py:414
  139.3 0.0 copy-start
  139.3 1.9 %copy.18 = bf16[1,64,3584]{2,1,0:T(8,128)(2,1)} copy(bf16[1,64,3584]{2,1,0:T(8,128)(2,1)} %bitcast.25) | data formatting | bytes 917504
  141.2 0.0 copy-done
  141.2 0.8 copy.19
Async XLA Ops:
  139.3 1.9 %copy-start = (bf16[64,3584]{1,0:T(8,128)(2,1)S(1)}, bf16[64,3584]{1,0:T(8,128)(2,1)}, u32[]{:S(2)}) copy-start(bf16[64,3584]{1,0:T(8,128)(2,1)} %get-tuple-element.5) | copy-start | bytes 1376260

commit v5 on v4

--- a/solution.py
+++ b/solution.py
@@ -40,7 +40,7 @@
            pbuf, ra, rb, rsend, ret,
            w_ss, w_rs, y_ss, y_rs, za_ss, za_rs, zb_ss, zb_rs, va_ss, va_rs, vb_ss, vb_rs, e_ss, e_rs,
            ra_ss, ra_rs, rb_ss, rb_rs, t_ss, t_rs, s_ss, s_rs, d_ss, d_rs,
-           dsend, drecv, pk0, pk1, scales, l_sem):
+           dsend, drecv, pk0, pk1, scales):
     sec = lax.axis_index("section")
     me = lax.axis_index("expert")
     y = me // NZ
@@ -107,13 +107,6 @@
             remote(dn_in.at[:, away], dnf.at[par], w_ss.at[1], w_rs.at[1], mate),
         )
 
-    def own_weights():
-        mine = pl.ds(pl.multiple_of(par * W, 128), W)
-        return (
-            pltpu.make_async_copy(up_in.at[par], upf.at[par], l_sem.at[0]),
-            pltpu.make_async_copy(dn_in.at[:, mine], dnf.at[par], l_sem.at[1]),
-        )
-
     def shift_copies(c):
         return (
             remote(shout.at[0, c], land.at[0, c], s_ss.at[0, c], s_rs.at[0, c], me, sec_up),
@@ -136,8 +129,6 @@
             if h < 2:
                 save_b(h + 1).start()
 
-    for copy in own_weights():
-        copy.start()
     earlier = (lax.broadcasted_iota(jnp.int32, (TOK, TOK), 0)
                < lax.broadcasted_iota(jnp.int32, (TOK, TOK), 1)).astype(F32).astype(BF)
     wide = lax.broadcasted_iota(jnp.int32, (WINDOW * PAD, TOK), 0)
@@ -239,7 +230,17 @@
             if t == 0 and c == 0:
                 for copy in weight_copies():
                     copy.start()
-        if t == 1:
+        if t == 0:
+            @pl.when(par == 0)
+            def _():
+                upf[0] = up_in[0]
+                dnf[0] = dn_in[:, :W]
+
+            @pl.when(par == 1)
+            def _():
+                upf[1] = up_in[1]
+                dnf[1] = dn_in[:, W:]
+        else:
             save_hop(3)
 
         def pre_half(b):
@@ -306,7 +307,6 @@
                         go_b(h + 1, c).start()
             if t == 0 and h == 1:
                 weight_copies()[0].wait()
-                own_weights()[0].wait()
                 upc[:, :HID_DEV] = upf[0]
                 upc[:, HID_DEV:] = upf[1]
                 for b in [z] + landed(0):
@@ -316,13 +316,12 @@
                     pre_half(b)
             if t == 0 and h == 2:
                 weight_copies()[1].wait()
-                own_weights()[1].wait()
                 for b in [z] + landed(0) + landed(1):
                     grad_half(b)
             if t == 1 or h >= 2:
                 for b in landed(h):
                     grad_half(b)
-            if h == 2:
+            if h == 3:
                 first_b = at(z - sgn * 3)
                 second_half(first_b)
                 for c in range(2):
@@ -414,7 +413,7 @@
     out, dx = pl.pallas_call(
         kernel,
         out_shape=(shape, shape),
-        in_specs=[vmem] * 5 + [pl.BlockSpec(memory_space=pl.ANY)] * 2 + [vmem] * 7,
+        in_specs=[vmem] * 14,
         out_specs=(vmem, vmem),
         scratch_shapes=[
             pltpu.VMEM((2, 2, 2, TOK, C), BF),
@@ -454,7 +453,6 @@
             pltpu.VMEM((4, WINDOW * PAD, TOK), BF),
             pltpu.VMEM((2, WINDOW * 8, TOK), BF),
             pltpu.VMEM((S, 2, 3, TOK, WINDOW * 8), BF),
-            dma((2,)),
         ],
         compiler_params=pltpu.CompilerParams(
             collective_id=0, has_side_effects=True, vmem_limit_bytes=60 * 1024 * 1024),

time: 142 us -> 138 us (0.972)
  Pallas kernels: 139 us -> 135 us
    pallas_call x1, Pallas kernels: 139 us -> 135 us  [local(): pl.pallas_call(kernel, out_shape=(shape, shape), in_specs=[vmem] * 14, ou...]
where the time goes in v5:
time: 138 us
  Pallas kernels  135 us (98%)
  local copies, waits for them, and re-layouts  2.64 us (2%)
    pallas_call x1, Pallas kernels, local(): pl.pallas_call(kernel, out_shape=(shape, shape), in_specs=[vmem] * 14, ou...  135 us

profile of v5, /device:TPU:6, one launch (start us, length us, event | category | flops | bytes accessed | tf_op | source)
XLA Modules:
  0.0 138.2 jit_solution(5274743693791676643)
XLA Ops:
  0.6 134.9 %shard_map.149 = (bf16[64,3584]{1,0:T(8,128)(2,1)}, bf16[64,3584]{1,0:T(8,128)(2,1)}) custom-call(bf16[64,3584]{1,0:T(8,128)(2,1)} %bitcast.26, bf16[64,3584]{1,0:T(8,128)(2,1)} %bitcast.27, bf16[2,64,3584]{2,1,0:T(8,128)(2,1)} %bitcast.21, bf16[64,3584]{1,0:T(8,128)(2,1)} %bitcast.28, bf16[64,3584]{1,0:T(8,128)(2,1)} %bitcast.29, ...), custom_call_target="tpu_custom_call" | custom-call | tf_op jit(solution)/shard_map/pallas_call | solution.py:413
  135.5 0.0 copy-start
  135.5 1.9 %copy.18 = bf16[1,64,3584]{2,1,0:T(8,128)(2,1)} copy(bf16[1,64,3584]{2,1,0:T(8,128)(2,1)} %bitcast.25) | data formatting | bytes 917504
  137.4 0.0 copy-done
  137.4 0.8 copy.19
Async XLA Ops:
  135.5 1.9 %copy-start = (bf16[64,3584]{1,0:T(8,128)(2,1)S(1)}, bf16[64,3584]{1,0:T(8,128)(2,1)}, u32[]{:S(2)}) copy-start(bf16[64,3584]{1,0:T(8,128)(2,1)} %get-tuple-element.5) | copy-start | bytes 1376260
